TPU v7x, 32 devices: a whole 2x2x4 slice. The times are simulated.
32 devices in a mesh: wide: 8 (over z, x), narrow: 4 (over y, core).
Axes of the slice: x: 2, y: 2, z: 4, core: 2. Of those that a mesh axis runs over, the one named last changes fastest.
Arguments:
- patches: bfloat16 [16384, 768], P(('wide', 'narrow')), may hold values from -6 to 6
- cotangent: bfloat16 [16384, 768], P(('wide', 'narrow')), may hold values from -6 to 6
- item_len: int32 [8, 4], P('wide'), may hold values from 0 to 2048, as said below
- valid_count: int32 [8, 4], P('wide'), may hold values from 0 to 2048, as said below
- norm1_gain: bfloat16 [768], P('wide'), may hold values from 0.5 to 1.5
- query_weight: bfloat16 [768, 768], P('wide', 'narrow'), may hold values from -0.0546875 to 0.0546875
- key_weight: bfloat16 [768, 768], P('wide', 'narrow'), may hold values from -0.21875 to 0.21875
- value_weight: bfloat16 [768, 768], P('wide', 'narrow'), may hold values from -0.21875 to 0.21875
- out_weight: bfloat16 [768, 768], P('narrow', 'wide'), may hold values from -1.75 to 1.75
- norm2_gain: bfloat16 [768], P('wide'), may hold values from 0.5 to 1.5
- gate_weight: bfloat16 [768, 2048], P('wide', 'narrow'), may hold values from -0.21875 to 0.21875
- up_weight: bfloat16 [768, 2048], P('wide', 'narrow'), may hold values from -0.21875 to 0.21875
- down_weight: bfloat16 [2048, 768], P('narrow', 'wide'), may hold values from -0.25 to 0.25
Outputs:
- output: bfloat16 [16384, 768], P(('wide', 'narrow'))
- grad_input: float32 [16384, 768], P(('wide', 'narrow'))
- grad_norm1: float32 [768], P('wide')
- grad_query: float32 [768, 768], P('wide', 'narrow')
- grad_key: float32 [768, 768], P('wide', 'narrow')
- grad_value: float32 [768, 768], P('wide', 'narrow')
- grad_out: float32 [768, 768], P('narrow', 'wide')
- grad_norm2: float32 [768], P('wide')
- grad_gate: float32 [768, 2048], P('wide', 'narrow')
- grad_up: float32 [768, 2048], P('wide', 'narrow')
- grad_down: float32 [2048, 768], P('narrow', 'wide')
Inputs may be any that keep to these rules, and one draw needn't show every extreme that they name: `item_len`: each row sums to 2048; its nonzero entries, each 512, 1024 or 2048, come before its zeros; some row is a single item of 2048. `valid_count`: each entry lies between half the matching item_len (rounded up) and that item_len; 0 for an empty slot; some item is wholly valid.
All inputs are finite; a program needn't handle non-finite values.
Results may differ from a plain program's by a relative error of at most 0.02.
Values may be sent and summed in bfloat16 or wider, within the bound.
No kernel may reach another device: no remote copies, remote signals or barrier semaphores. Data moves between devices by JAX's collectives and lax.ppermute only.
A program may use at most 192 MiB of HBM per device.

v0:
```python
import functools

import jax
import jax.numpy as jnp
from jax import lax
from jax.experimental import pallas as pl
from jax.experimental.pallas import tpu as pltpu
from jax.sharding import PartitionSpec as P

HEAD = 64
BUCKET = 2048
EPSILON = 1e-06
MASKED = -1e30
NARROW = 4


NT = (((1,), (1,)), ((), ()))
NN = (((1,), (0,)), ((), ()))
TN = (((0,), (0,)), ((), ()))


def dot(left, right, dims=NN):
    return lax.dot_general(left, right, dims, preferred_element_type=jnp.float32)


def low(values):
    return values.astype(jnp.bfloat16)


def wide32(values):
    return values.astype(jnp.float32)


def swap(values, axis, bits):
    size = lax.axis_size(axis)
    return lax.ppermute(values, axis, [(i, i ^ bits) for i in range(size)])


def after(values, *earlier):
    return lax.optimization_barrier((values, *earlier))[0]


def gather_rows(own):
    across = swap(own, "narrow", 2)
    return own, swap(own, "narrow", 1), across, swap(across, "narrow", 1)


def pair_sum(parts):
    return wide32(parts[0]) + wide32(swap(parts[1], "narrow", 1))


def cross(values):
    return wide32(swap(low(values), "narrow", 2))


def places():
    if lax.axis_size("wide") != 8:
        return jnp.arange(8, dtype=jnp.int32)
    index = lax.axis_index("wide").astype(jnp.int32)
    order = jnp.array([0, 2, 4, 6, 1, 3, 5, 7], jnp.int32)
    return jnp.bitwise_xor(order, index)


def gather_wide(own, ready=()):
    if lax.axis_size("wide") != 8:
        return jnp.split(lax.all_gather(own, "wide", axis=0, tiled=True), 8, axis=0)
    column = [own] + [swap(own, "wide", 2 * k) for k in (1, 2, 3)]
    sent = [after(own, *ready)] + column[1:]
    return column + [swap(piece, "wide", 1) for piece in sent]


def send_x(sent):
    if lax.axis_size("wide") != 8:
        return sent
    return [swap(part, "wide", 1) for part in sent]


def add_x(kept, received):
    rows = kept[0].shape[0]
    far = [received[0][j * rows : (j + 1) * rows] for j in range(3)]
    return [low(wide32(mine) + wide32(other)) for mine, other in zip(kept, [received[1]] + far[::-1])]


def send_z(column):
    return [column[0]] + [swap(column[k], "wide", 2 * k) for k in (3, 2, 1)]


def reduce_wide(parts):
    size = lax.axis_size("wide")
    if size == 8:
        columns = [add_x(kept, received) for kept, received in parts]
        return send_z([jnp.concatenate(pieces, axis=1) for pieces in zip(*columns)])
    full = []
    for kept, sent in parts:
        rows = kept[0].shape[0]
        far = [sent[0][j * rows : (j + 1) * rows] for j in range(3)]
        full.append(jnp.concatenate(kept + [sent[1]] + far[::-1], axis=0))
    full = jnp.concatenate(full, axis=1)
    return list(lax.all_to_all(full.reshape(size, -1, full.shape[1]), "wide", 0, 0, tiled=True))


def sum_all(values):
    values = values + swap(values, "narrow", 1)
    values = values + swap(values, "narrow", 2)
    size = lax.axis_size("wide")
    if size != 8:
        values = lax.psum(values, "wide")
    else:
        for bits in (1, 2, 4):
            values = values + swap(values, "wide", bits)
    rows = values.shape[1] // size
    return lax.dynamic_slice_in_dim(values, lax.axis_index("wide") * rows, rows, 1)


def call(kernel, grid, in_specs, out_specs, out_shape, scratch=(), prefetch=0):
    return pl.pallas_call(
        kernel,
        out_shape=out_shape,
        grid_spec=pltpu.PrefetchScalarGridSpec(
            num_scalar_prefetch=prefetch,
            grid=grid,
            in_specs=in_specs,
            out_specs=out_specs,
            scratch_shapes=scratch,
        ),
        compiler_params=pltpu.CompilerParams(
            dimension_semantics=("arbitrary",) * len(grid), vmem_limit_bytes=52 << 20
        ),
    )


def by_row(block, width):
    return pl.BlockSpec((block, width), lambda i, *_: (i, 0))


def whole(*shape):
    return pl.BlockSpec(shape, lambda i, *_: (0,) * len(shape))


def shaped(shape, dtype=jnp.bfloat16):
    return jax.ShapeDtypeStruct(shape, dtype)


def inverse_rms(values):
    return lax.rsqrt(jnp.mean(values * values, axis=-1, keepdims=True) + EPSILON)


def eight(values):
    return jnp.sum(values.reshape(values.shape[0] // 8, 8, values.shape[1]), axis=0)


def parts_in(parts, block):
    per = parts[0].shape[0] // block
    width = parts[0].shape[1]

    def spec(j):
        return pl.BlockSpec((block, width), lambda i, *_: (jnp.clip(i - j * per, 0, per - 1), 0))

    return [spec(j) for j in range(len(parts))]


def pick(refs, steps):
    value = refs[0][...]
    for j in range(1, len(refs)):
        value = jnp.where(pl.program_id(0) >= j * (steps // len(refs)), refs[j][...], value)
    return value


def halves(block, width, steps):
    per = steps // 2
    return [
        pl.BlockSpec((block, width), lambda i, *_: (jnp.minimum(i, per - 1), 0)),
        pl.BlockSpec((block, width), lambda i, *_: (jnp.maximum(i - per, 0), 0)),
    ]


def put(refs, value, steps):
    @pl.when(pl.program_id(0) < steps // 2)
    def _():
        refs[0][...] = value

    @pl.when(pl.program_id(0) >= steps // 2)
    def _():
        refs[1][...] = value


def eye(size):
    return low(
        wide32(lax.broadcasted_iota(jnp.int32, (size, size), 0) == lax.broadcasted_iota(jnp.int32, (size, size), 1))
    )


def pack_kernel(q_ref, k_ref, v_ref, o_ref, g1_ref, g2_ref, gate_ref, up_ref, down_ref, a_ref, b_ref):
    rows, width = q_ref.shape
    hidden = gate_ref.shape[1]
    one = eye(rows)
    a_ref[:, :width] = q_ref[...]
    a_ref[:, width : 2 * width] = k_ref[...]
    a_ref[:, 2 * width : 3 * width] = v_ref[...]
    a_ref[:, 3 * width : 4 * width] = low(dot(one, o_ref[...], NT))
    line = lax.broadcasted_iota(jnp.int32, (a_ref.shape[1] - 4 * width, rows), 0)
    gains = jnp.where(line == 0, wide32(g1_ref[...]), jnp.where(line == 1, wide32(g2_ref[...]), 0.0))
    a_ref[:, 4 * width :] = low(dot(one, low(gains), NT))
    b_ref[:, :hidden] = gate_ref[...]
    b_ref[:, hidden : 2 * hidden] = up_ref[...]
    b_ref[:, 2 * hidden :] = down_ref[...]


def round_up(count):
    return -(-count // 128) * 128


def pack(q, k, v, o, gain_one, gain_two, gate, up, down):
    rows, width = q.shape
    first, second = round_up(4 * width + 2), 3 * gate.shape[1]
    if lax.axis_size("wide") != 8:
        a = jnp.concatenate([q, k, v, o.T, gain_one[:, None], gain_two[:, None]], axis=1)
        return jnp.pad(a, ((0, 0), (0, first - a.shape[1]))), jnp.concatenate([gate, up, down], axis=1)
    args = (q, k, v, o, gain_one[None], gain_two[None], gate, up, down)
    return call(
        pack_kernel,
        (1,),
        [whole(*arg.shape) for arg in args],
        [whole(rows, first), whole(rows, second)],
        [shaped((rows, first)), shaped((rows, second))],
    )(*args)


def lay(place_ref, pieces, target):
    rows = pieces[0].shape[0]
    for j, piece in enumerate(pieces):
        target[pl.ds(pl.multiple_of(place_ref[j] * rows, 32), rows), :] = piece[...]


def project_kernel(place_ref, *refs, width, steps):
    xs, ws, (h_ref, q_ref, k_ref, v_ref, w_ref, out_ref, gain_ref) = refs[:4], refs[4:12], refs[12:]

    @pl.when(pl.program_id(0) == 0)
    def _():
        lay(place_ref, ws, w_ref)
        out_ref[...] = w_ref[:, 3 * width : 4 * width]
        gain_ref[...] = wide32(w_ref[:, 4 * width : 4 * width + 128]).T[:8]

    x = wide32(pick(xs, steps))
    h = low(x * inverse_rms(x) * gain_ref[0:1, :])
    h_ref[...] = h
    qkv = low(dot(h, w_ref[:, : 3 * width]))
    q_ref[...] = qkv[:, :width]
    k_ref[...] = qkv[:, width : 2 * width]
    v_ref[...] = qkv[:, 2 * width :]


def project(place, rows, pieces, width, block=512):
    d, full = rows[0].shape[1], pieces[0].shape[1]
    tokens = 4 * rows[0].shape[0]
    steps = tokens // block
    return call(
        functools.partial(project_kernel, width=width, steps=steps),
        (steps,),
        parts_in(rows, block) + [whole(*piece.shape) for piece in pieces],
        [by_row(block, d)] + [by_row(block, width)] * 3 + [whole(d, full), whole(d, width), whole(8, d)],
        [shaped((tokens, d))] + [shaped((tokens, width))] * 3 + [shaped((d, full)), shaped((d, width)), shaped((8, d), jnp.float32)],
        prefetch=1,
    )(place, *rows, *pieces)


def grads_kernel(place_ref, *refs, groups, steps):
    kept, (far, fourth), total = refs[-7:-3], refs[-3:-1], refs[-1]
    refs = list(refs[:-7])
    step = pl.program_id(0)

    def take(count):
        taken = refs[:count]
        del refs[:count]
        return pick(taken, steps)

    found = []
    for lhs_parts, rhs_parts in groups:
        lhs = take(lhs_parts)
        found.append(dot(lhs, jnp.concatenate([take(count) for count in rhs_parts], axis=1), TN))

    @pl.when(step == 0)
    def _():
        total[...] = jnp.concatenate(found, axis=1)

    @pl.when(step > 0)
    def _():
        total[...] += jnp.concatenate(found, axis=1)

    @pl.when(step == steps - 1)
    def _():
        rows = fourth.shape[0]

        def piece(j):
            return low(total[pl.ds(pl.multiple_of(place_ref[j] * rows, 32), rows), :])

        for j in range(4):
            kept[j][...] = piece(j)
        for j in range(3):
            far[j * rows : (j + 1) * rows, :] = piece(7 - j)
        fourth[...] = piece(4)


def grad_pieces(place, groups, block=512):
    arrays, counts, specs, full = [], [], [], 0
    for lhs, rhs in groups:
        counts.append((len(lhs), [len(parts) for parts in rhs]))
        for parts in [lhs] + rhs:
            arrays += parts
            specs += parts_in(parts, block)
        full += sum(parts[0].shape[1] for parts in rhs)
    tokens = sum(part.shape[0] for part in groups[0][0])
    d = groups[0][0][0].shape[1]
    shapes = [(d // 8, full)] * 4 + [(3 * d // 8, full), (d // 8, full)]
    found = call(
        functools.partial(grads_kernel, groups=counts, steps=tokens // block),
        (tokens // block,),
        specs,
        [whole(*shape) for shape in shapes],
        [shaped(shape) for shape in shapes],
        scratch=[pltpu.VMEM((d, full), jnp.float32)],
        prefetch=1,
    )(place, *arrays)
    return list(found[:4]), list(found[4:])


def finish_kernel(*refs, widths):
    pieces, outs = refs[: -len(widths)], refs[-len(widths) :]
    total = wide32(pieces[0][...])
    for piece in pieces[1:]:
        total = total + wide32(piece[...])
    at = 0
    for out, width in zip(outs, widths):
        part = total[:, at : at + width]
        out[...] = part.T if out.shape[1] == part.shape[0] else part
        at += width


def finish(pieces, widths, turned):
    if len(pieces) != 4:
        cuts = [sum(widths[: j + 1]) for j in range(len(widths) - 1)]
        parts = jnp.split(sum(wide32(piece) for piece in pieces), cuts, 1)
        return (*parts[:-1], parts[-1].T) if turned else parts
    rows, full = pieces[0].shape
    shapes = [(rows, width) for width in widths[:-1]] + [(widths[-1], rows) if turned else (rows, widths[-1])]
    return call(
        functools.partial(finish_kernel, widths=widths),
        (1,),
        [whole(rows, full)] * 4,
        [whole(*shape) for shape in shapes],
        [shaped(shape, jnp.float32) for shape in shapes],
    )(*pieces)


def key_bias(len_ref, cnt_ref, own_ref, row, items):
    unit = BUCKET // NARROW
    own = own_ref[0]
    col = lax.broadcasted_iota(jnp.int32, (1, BUCKET), 1)
    col = ((col // unit) ^ own) * unit + col % unit
    row = ((row // unit) ^ own) * unit
    start = jnp.int32(0)
    low_end = jnp.int32(0)
    high_end = jnp.int32(0)
    for i in range(items):
        length = len_ref[0, i]
        inside = (row >= start) & (row < start + length)
        low_end = jnp.where(inside, start, low_end)
        high_end = jnp.where(inside, start + cnt_ref[0, i], high_end)
        start = start + length
    return jnp.where((col >= low_end) & (col < high_end), 0.0, MASKED).astype(jnp.float32)


def forward_kernel(
    len_ref, cnt_ref, own_ref, q_ref, k_ref, v_ref, o_ref, lse_ref, *, first, block, heads, items
):
    bias = key_bias(len_ref, cnt_ref, own_ref, first + pl.program_id(0) * block, items)
    for h in range(heads):
        cols = slice(h * HEAD, (h + 1) * HEAD)
        scores = dot(q_ref[:, cols], k_ref[:, cols], NT) + bias
        highest = jnp.max(scores, axis=-1, keepdims=True)
        weights = jnp.exp(scores - highest)
        total = jnp.sum(weights, axis=-1, keepdims=True)
        o_ref[:, cols] = low(dot(low(weights), v_ref[:, cols]) / total)
        lse_ref[:, h : h + 1] = highest + jnp.log(total)


def attention_forward(scalars, q, k, v, first, block=256):
    tokens, width = q.shape
    heads, items = width // HEAD, scalars[0].shape[1]
    rows = tokens // 2
    at = first // block
    row = pl.BlockSpec((block, width), lambda i, *_: (i + at, 0))
    return call(
        functools.partial(forward_kernel, first=first, block=block, heads=heads, items=items),
        (rows // block,),
        [row, whole(tokens, width), whole(tokens, width)],
        [by_row(block, width), by_row(block, heads)],
        [shaped((rows, width)), shaped((rows, heads), jnp.float32)],
        prefetch=3,
    )(*scalars, q, k, v)


def backward_kernel(
    len_ref, cnt_ref, own_ref, q_ref, k_ref, v_ref, ga_ref, gb_ref, w_ref, o_ref, lse_ref, *rest, first, block, heads, items, steps
):
    if first:
        dk_in, dv_in, dq_ref, dk_ref, dv_ref, dk_sum, dv_sum = rest
    else:
        dq_ref, dk_sum, dv_sum = rest
    step = pl.program_id(0)
    bias = key_bias(len_ref, cnt_ref, own_ref, first + step * block, items)

    @pl.when(step == 0)
    def _():
        dk_sum[...] = dk_in[...] if first else jnp.zeros_like(dk_sum)
        dv_sum[...] = dv_in[...] if first else jnp.zeros_like(dv_sum)

    do_all = low(dot(pick((ga_ref, gb_ref), steps), w_ref[:, : heads * HEAD]))
    for h in range(heads):
        cols = slice(h * HEAD, (h + 1) * HEAD)
        q, k, v, do = q_ref[:, cols], k_ref[:, cols], v_ref[:, cols], do_all[:, cols]
        delta = jnp.sum(wide32(do) * wide32(o_ref[:, cols]), axis=-1, keepdims=True)
        probs = jnp.exp(dot(q, k, NT) + bias - lse_ref[:, h : h + 1])
        ds = low(probs * (dot(do, v, NT) - delta))
        dq_ref[:, cols] = low(dot(ds, k))
        dv_sum[cols, :] += dot(do, low(probs), TN)
        dk_sum[cols, :] += dot(q, ds, TN)

    if first:

        @pl.when(step == pl.num_programs(0) - 1)
        def _():
            dk_ref[...] = low(dk_sum[...].T)
            dv_ref[...] = low(dv_sum[...].T)


def attention_backward(scalars, q, k, v, grad, out_w, o, lse, sums, block=128):
    tokens, width = q.shape
    heads, items = width // HEAD, scalars[0].shape[1]
    rows = tokens // 2
    first = rows if sums else 0
    at = first // block
    row = pl.BlockSpec((block, width), lambda i, *_: (i + at, 0))
    full = whole(tokens, width)
    turned = whole(width, tokens)
    kept = shaped((width, tokens), jnp.float32)
    in_specs = [row, full, full] + parts_in(grad, block) + [whole(*out_w.shape), by_row(block, width), by_row(block, heads)]
    return call(
        functools.partial(backward_kernel, first=first, block=block, heads=heads, items=items, steps=rows // block),
        (rows // block,),
        in_specs + ([turned, turned] if sums else []),
        [by_row(block, width)] + ([full, full] if sums else [turned, turned]),
        [shaped((rows, width))] + ([shaped((tokens, width))] * 2 if sums else [kept, kept]),
        scratch=[pltpu.VMEM((width, tokens), jnp.float32)] * 2 if sums else [],
        prefetch=3,
    )(*scalars, q, k, v, *grad, out_w, o, lse, *sums)


def mlp_kernel(place_ref, *refs, width, heads_width, steps, near):
    xs, gs, os, ws, gain_ref = refs[:2], refs[2:4], refs[4:8], refs[8:12], refs[12]
    pieces, outs = (refs[13:14], refs[14:]) if near else (refs[13:21], refs[21:])
    ys, dhs, (h_ref, hid_ref, dg_ref, du_ref, norm_ref) = outs[:2], outs[2:4], outs[4:9]
    w_ref = pieces[0] if near else outs[9]
    if not near:

        @pl.when(pl.program_id(0) == 0)
        def _():
            lay(place_ref, pieces, w_ref)

    m = wide32(pick(xs, steps))
    for o_ref, out_ref in zip(os, ws):
        m = m + dot(o_ref[...], out_ref[:, :heads_width], NT)
    if near:

        @pl.when(pl.program_id(0) < steps // 2)
        def _():
            outs[9][...] = m

    n = m * inverse_rms(m)
    h = low(n * gain_ref[1:2, :])
    h_ref[...] = h
    both = dot(h, w_ref[:, : 2 * width])
    gate, up = both[:, :width], both[:, width:]
    square = gate * gate
    scale = 0.7978845608028654
    t = jnp.tanh(scale * gate * (1.0 + 0.044715 * square))
    half = 0.5 * (1.0 + t)
    act = gate * half
    slope = half + (0.5 * scale) * gate * (1.0 - t * t) * (1.0 + 0.134145 * square)
    hid = low(act * up)
    hid_ref[...] = hid
    put(ys, low(dot(hid, w_ref[:, 2 * width :], NT)), steps)
    dhid = dot(pick(gs, steps), w_ref[:, 2 * width :])
    dgate = low(dhid * up * slope)
    dup = low(dhid * act)
    dg_ref[...] = dgate
    du_ref[...] = dup
    dh = dot(dgate, w_ref[:, :width], NT) + dot(dup, w_ref[:, width : 2 * width], NT)
    put(dhs, low(dh), steps)

    @pl.when(pl.program_id(0) == 0)
    def _():
        norm_ref[...] = jnp.zeros_like(norm_ref)

    norm_ref[...] += eight(dh * n)


def mlp(place, xs, gs, os, out_ws, gains, weight, near, block=256):
    part, d = xs[0].shape
    rows, steps = 2 * part, 2 * part // block
    width, heads_width = weight[0].shape[1] // 3, os[0].shape[1]
    wide_row, thin_row = by_row(block, d), by_row(block, width)
    split = halves(block, d, steps)
    other = pl.BlockSpec((block, heads_width), lambda i, *_: ((i + steps // 2) % steps, 0))
    out = call(
        functools.partial(mlp_kernel, width=width, heads_width=heads_width, steps=steps, near=near),
        (steps,),
        parts_in(xs, block) + parts_in(gs, block) + [by_row(block, heads_width), other] * 2
        + [whole(*out_ws[0].shape)] * 4 + [whole(8, d)] + [whole(*piece.shape) for piece in weight],
        split * 2 + [wide_row] + [thin_row] * 3 + [whole(8, d)] + (split[:1] if near else [whole(d, 3 * width)]),
        [shaped((part, d))] * 4 + [shaped((rows, d))] + [shaped((rows, width))] * 3
        + [shaped((8, d), jnp.float32)] + [shaped((part, d), jnp.float32) if near else shaped((d, 3 * width))],
        prefetch=1,
    )(place, *xs, *gs, *os, *out_ws, gains, *weight)
    return (out[:2], out[2:4]) + tuple(out[4:])


def rows_kernel(dq_ref, dk_ref, dv_ref, xa_ref, xb_ref, w_ref, dha_ref, dhb_ref, norm_ref, *, width, steps):
    dh = dot(dq_ref[...], w_ref[:, :width], NT)
    dh += dot(dk_ref[...], w_ref[:, width : 2 * width], NT)
    dh += dot(dv_ref[...], w_ref[:, 2 * width : 3 * width], NT)
    put((dha_ref, dhb_ref), low(dh), steps)
    x = wide32(pick((xa_ref, xb_ref), steps))

    @pl.when(pl.program_id(0) == 0)
    def _():
        norm_ref[...] = jnp.zeros_like(norm_ref)

    norm_ref[...] += eight(dh * x * inverse_rms(x))


def rows_back(dq, dk, dv, xs, weight, first, block=256):
    count, width = dq.shape
    part, d = xs[0].shape
    at, steps = first // block, count // block
    late = pl.BlockSpec((block, width), lambda i, *_: (i + at, 0))
    dha, dhb, norm = call(
        functools.partial(rows_kernel, width=width, steps=steps),
        (steps,),
        [by_row(block, width), late, late] + parts_in(xs, block) + [whole(*weight.shape)],
        halves(block, d, steps) + [whole(8, d)],
        [shaped((part, d))] * 2 + [shaped((8, d), jnp.float32)],
    )(dq, dk, dv, *xs, weight)
    return (dha, dhb), norm


def norm_back(values, gain, grad):
    r = inverse_rms(values)
    n = values * r
    scaled = gain * grad
    return r * (scaled - n * jnp.mean(scaled * n, axis=-1, keepdims=True))


def on_device(
    patches, cotangent, item_len, valid_count, norm1_gain, query_weight, key_weight, value_weight,
    out_weight, norm2_gain, gate_weight, up_weight, down_weight,
):
    width = query_weight.shape[1]
    hidden = gate_weight.shape[1]
    scalars = (item_len, valid_count, lax.axis_index("narrow").astype(jnp.int32).reshape(1))
    place = places()
    attn_own, mlp_own = pack(
        query_weight, key_weight, value_weight, out_weight, norm1_gain, norm2_gain,
        gate_weight, up_weight, down_weight.T,
    )
    x = gather_rows(patches)
    attn_pieces = gather_wide(attn_own)
    mlp_pieces = gather_wide(after(mlp_own, *attn_pieces[1:4]), attn_pieces[4:])
    g = gather_rows(after(cotangent, *attn_pieces[1:4]))

    h_one, q, k, v, qkv_w, out_w, gains = project(place, x, attn_pieces, width)
    out_ws = gather_rows(after(out_w, g[2]))
    half = q.shape[0] // 2
    o_near, lse_near = attention_forward(scalars, q, k, v, 0)
    o_far_across = swap(o_near, "narrow", 2)
    o_far_across = (o_far_across, swap(o_far_across, "narrow", 1))
    o_far, lse_far = attention_forward(scalars, q, k, v, half)
    o_near_across = swap(o_far, "narrow", 2)
    o_far_all = (o_far, swap(o_far, "narrow", 1)) + o_far_across
    o_near_all = (o_near, swap(o_near, "narrow", 1), o_near_across, swap(o_near_across, "narrow", 1))
    y_far, dh_far, h2_far, hid_far, dg_far, du_far, n2_far, mlp_w = mlp(
        place, x[2:], g[2:], o_far_all, out_ws, gains, mlp_pieces, False
    )
    from_far = cross(pair_sum(dh_far))
    y_near, dh_near, h2_near, hid_near, dg_near, du_near, n2_near, middle_own = mlp(
        place, x[:2], g[:2], o_near_all, out_ws, gains, [mlp_w], True
    )
    gain_one, gain_two = gains[0:1], gains[1:2]
    dh_two = pair_sum(dh_near) + from_far
    mlp_parts = grad_pieces(
        place,
        [([h2_near, h2_far], [[dg_near, dg_far], [du_near, du_far]]), (list(g), [[hid_near, hid_far]])],
    )
    mlp_sent = send_x(mlp_parts[1])
    middle_grad_own = wide32(cotangent) + norm_back(middle_own, gain_two, dh_two)
    d = gather_rows(low(middle_grad_own))
    grad_gate, grad_up, grad_down = finish(reduce_wide([(mlp_parts[0], mlp_sent)]), (hidden, hidden, hidden), False)
    dq_near, dk_sum, dv_sum = attention_backward(scalars, q, k, v, d[:2], out_w, o_near, lse_near, ())
    output = low(middle_own + pair_sum(y_near) + cross(after(pair_sum(y_far), d[2])))
    out_parts = grad_pieces(place, [(list(d), [[o_near, o_far]])])
    out_sent = send_x(out_parts[1])
    dq_far, dk, dv = attention_backward(scalars, q, k, v, d[2:], out_w, o_far, lse_far, (dk_sum, dv_sum))
    attn_parts = grad_pieces(place, [([h_one], [[dq_near, dq_far], [dk], [dv]])])
    attn_sent = send_x(attn_parts[1])
    dh_far, n1_far = rows_back(dq_far, dk, dv, x[2:], qkv_w, half)
    from_far = cross(pair_sum(dh_far))
    dh_near, n1_near = rows_back(dq_near, dk, dv, x[:2], qkv_w, 0)
    grad_query, grad_key, grad_value, grad_out = finish(
        reduce_wide([(attn_parts[0], attn_sent), (out_parts[0], out_sent)]), (width, width, width, width), True
    )
    dh_one = pair_sum(dh_near) + from_far
    grad_input = middle_grad_own + norm_back(wide32(patches), gain_one, dh_one)
    norms = sum_all(
        jnp.stack([jnp.sum(n1_near + n1_far, axis=0), jnp.sum(n2_near + n2_far, axis=0)], axis=0)
    )
    return (
        output, grad_input, norms[0], grad_query, grad_key, grad_value, grad_out, norms[1],
        grad_gate, grad_up, grad_down.T,
    )


def solution(mesh):
    tokens = P(("wide", "narrow"), None)

    return jax.shard_map(
        on_device,
        mesh=mesh,
        in_specs=(
            tokens, tokens, P("wide", None), P("wide", None), P("wide"), P("wide", "narrow"),
            P("wide", "narrow"), P("wide", "narrow"), P("narrow", "wide"), P("wide"),
            P("wide", "narrow"), P("wide", "narrow"), P("narrow", "wide"),
        ),
        out_specs=(
            tokens, tokens, P("wide"), P("wide", "narrow"), P("wide", "narrow"), P("wide", "narrow"),
            P("narrow", "wide"), P("wide"), P("wide", "narrow"), P("wide", "narrow"), P("narrow", "wide"),
        ),
        check_vma=False,
    )
```

profile of v0, /device:TPU:0, one launch (start us, length us, event | category | flops | bytes accessed | tf_op | source)
XLA Modules:
  0.0 356.1 jit_solution(7744489731387706102)
XLA Ops:
  11.2 3.7 %collective-permute-start.3 = (bf16[96,896]{1,0:T(8,128)(2,1)S(1)}, bf16[96,896]{1,0:T(8,128)(2,1)S(1)}, u32[]{:S(2)}, u32[]{:S(2)}) collective-permute-start(bf16[96,896]{1,0:T(8,128)(2,1)S(1)} %get-tuple-element.86.refs_4_), channel_id=1, source_target_pairs={{0,24},{4,28},{8,16},{12,20},{16,8},{20,12},{24,0},{28,4},{1,25},{... | collective-permute-start | bytes 516104 | tf_op jit(solution)/shard_map/ppermute | solution.py:36
  15.6 4.7 %collective-permute-done.3.refs_7_ = bf16[96,896]{1,0:T(8,128)(2,1)S(1)} collective-permute-done((bf16[96,896]{1,0:T(8,128)(2,1)S(1)}, bf16[96,896]{1,0:T(8,128)(2,1)S(1)}, u32[]{:S(2)}, u32[]{:S(2)}) %collective-permute-start.3) | collective-permute-done | bytes 172064 | tf_op jit(solution)/shard_map/ppermute | solution.py:36
  20.3 8.8 %collective-permute-done.2.refs_6_ = bf16[96,896]{1,0:T(8,128)(2,1)S(1)} collective-permute-done((bf16[96,896]{1,0:T(8,128)(2,1)S(1)}, bf16[96,896]{1,0:T(8,128)(2,1)S(1)}, u32[]{:S(2)}, u32[]{:S(2)}) %collective-permute-start.2) | collective-permute-done | bytes 172064 | tf_op jit(solution)/shard_map/ppermute | solution.py:36
  31.7 4.2 %collective-permute-done.7.refs_8_ = bf16[96,896]{1,0:T(8,128)(2,1)S(1)} collective-permute-done((bf16[96,896]{1,0:T(8,128)(2,1)S(1)}, bf16[96,896]{1,0:T(8,128)(2,1)S(1)}, u32[]{:S(2)}, u32[]{:S(2)}) %collective-permute-start.7) | collective-permute-done | bytes 172064 | tf_op jit(solution)/shard_map/ppermute | solution.py:36
  49.0 12.8 %collective-permute-start.22 = (bf16[96,1536]{1,0:T(8,128)(2,1)S(1)}, bf16[96,1536]{1,0:T(8,128)(2,1)S(1)}, u32[]{:S(2)}, u32[]{:S(2)}) collective-permute-start(bf16[96,1536]{1,0:T(8,128)(2,1)S(1)} %get-tuple-element.98.refs_13_), channel_id=1, source_target_pairs={{0,8},{4,12},{8,0},{12,4},{16,24},{20,28},{24,16},{28,20},{1,9},{5... | collective-permute-start | bytes 884744 | tf_op jit(solution)/shard_map/ppermute | solution.py:36
  64.5 8.6 %shard_map.222 = (bf16[2048,768]{1,0:T(8,128)(2,1)}, bf16[2048,192]{1,0:T(8,128)(2,1)}, bf16[2048,192]{1,0:T(8,128)(2,1)}, bf16[2048,192]{1,0:T(8,128)(2,1)}, bf...) custom-call(s32[8]{0:T(128)S(1)} %broadcast_xor_fusion.place_ref, ...), custom_call_target="tpu_custom_call" | custom-call | tf_op jit(solution)/shard_map/pallas_call | solution.py:257
  73.1 13.4 %shard_map.223 = (bf16[1024,192]{1,0:T(8,128)(2,1)S(1)}, f32[1024,3]{1,0:T(8,128)S(1)}) custom-call(s32[1,4]{1,0:T(1,128)S(1)} %copy-done.22, s32[1,4]{1,0:T(1,128)S(1)} %copy-done.23, s32[1]{0:T(128)} %bitcast.3.own_ref, bf16[2048,192]{1,0:T(8,128)(2,1)} %get-tuple-element.88.q_ref, bf16[2048,192]{1,0:T(8,128)(2,1)} %get-tuple-element.89.k_ref, ...), custom_call_target="tpu_custom_call" | custom-call | tf_op jit(solution)/shard_map/pallas_call | solution.py:393
  90.6 13.4 %shard_map.224 = (bf16[1024,192]{1,0:T(8,128)(2,1)S(1)}, f32[1024,3]{1,0:T(8,128)S(1)}) custom-call(s32[1,4]{1,0:T(1,128)S(1)} %copy-done.22, s32[1,4]{1,0:T(1,128)S(1)} %copy-done.23, s32[1]{0:T(128)} %bitcast.3.own_ref, bf16[2048,192]{1,0:T(8,128)(2,1)} %get-tuple-element.88.q_ref, bf16[2048,192]{1,0:T(8,128)(2,1)} %get-tuple-element.89.k_ref, ...), custom_call_target="tpu_custom_call" | custom-call | tf_op jit(solution)/shard_map/pallas_call | solution.py:393
  104.8 4.5 %collective-permute-done.16.refs_10_ = bf16[768,192]{1,0:T(8,128)(2,1)S(1)} collective-permute-done((bf16[768,192]{1,0:T(8,128)(2,1)S(1)}, bf16[768,192]{1,0:T(8,128)(2,1)S(1)}, u32[]{:S(2)}, u32[]{:S(2)}) %collective-permute-start.16) | collective-permute-done | bytes 294944 | tf_op jit(solution)/shard_map/ppermute | solution.py:36
  112.5 17.4 %shard_map.225 = (bf16[512,768]{1,0:T(8,128)(2,1)}, bf16[512,768]{1,0:T(8,128)(2,1)}, bf16[512,768]{1,0:T(8,128)(2,1)}, bf16[512,768]{1,0:T(8,128)(2,1)}, bf16[1...) custom-call(s32[8]{0:T(128)S(1)} %broadcast_xor_fusion.place_ref, ...), custom_call_target="tpu_custom_call" | custom-call | tf_op jit(solution)/shard_map/pallas_call | solution.py:515
  137.8 17.1 %shard_map.226 = (bf16[512,768]{1,0:T(8,128)(2,1)}, bf16[512,768]{1,0:T(8,128)(2,1)}, bf16[512,768]{1,0:T(8,128)(2,1)}, bf16[512,768]{1,0:T(8,128)(2,1)}, bf16[1...) custom-call(s32[8]{0:T(128)S(1)} %broadcast_xor_fusion.place_ref, ...), custom_call_target="tpu_custom_call" | custom-call | tf_op jit(solution)/shard_map/pallas_call | solution.py:515
  157.5 17.7 %collective-permute-done.33 = bf16[512,768]{1,0:T(8,128)(2,1)S(1)} collective-permute-done((bf16[512,768]{1,0:T(8,128)(2,1)S(1)}, bf16[512,768]{1,0:T(8,128)(2,1)S(1)}, u32[]{:S(2)}, u32[]{:S(2)}) %collective-permute-start.33) | collective-permute-done | bytes 786464 | tf_op jit(solution)/shard_map/ppermute | solution.py:36
  179.2 18.0 %collective-permute-done.34.ga_ref.refs_2_ = bf16[512,768]{1,0:T(8,128)(2,1)S(1)} collective-permute-done((bf16[512,768]{1,0:T(8,128)(2,1)S(1)}, bf16[512,768]{1,0:T(8,128)(2,1)S(1)}, u32[]{:S(2)}, u32[]{:S(2)}) %collective-permute-start.34) | collective-permute-done | bytes 786464 | tf_op jit(solution)/shard_map/ppermute | solution.py:36
  197.7 12.4 %shard_map.234 = (bf16[96,1536]{1,0:T(8,128)(2,1)S(1)}, bf16[96,1536]{1,0:T(8,128)(2,1)S(1)}, bf16[96,1536]{1,0:T(8,128)(2,1)S(1)}, bf16[96,1536]{1,0:T(8,128)(2...) custom-call(s32[8]{0:T(128)S(1)} %broadcast_xor_fusion.place_ref, ...), custom_call_target="tpu_custom_call" | custom-call | tf_op jit(solution)/shard_map/pallas_call | solution.py:315
  213.5 21.9 %shard_map.227 = (bf16[1024,192]{1,0:T(8,128)(2,1)S(1)}, f32[192,2048]{1,0:T(8,128)}, f32[192,2048]{1,0:T(8,128)}) custom-call(s32[1,4]{1,0:T(1,128)S(1)} %copy-done.22, s32[1,4]{1,0:T(1,128)S(1)} %copy-done.23, s32[1]{0:T(128)} %bitcast.3.own_ref, bf16[2048,192]{1,0:T(8,128)(2,1)} %get-tuple-element.88.q_ref, bf16[2048,192]{1,0:T(8,128)(2,1)} %get-tuple-element.89.k_ref, ...), custom_call_target="tpu_custom_call" | custom-call | tf_op jit(solution)/shard_map/pallas_call | solution.py:448
  236.3 23.4 %shard_map.228 = (bf16[1024,192]{1,0:T(8,128)(2,1)S(1)}, bf16[2048,192]{1,0:T(8,128)(2,1)}, bf16[2048,192]{1,0:T(8,128)(2,1)}) custom-call(s32[1,4]{1,0:T(1,128)S(1)} %copy-done.22, s32[1,4]{1,0:T(1,128)S(1)} %copy-done.23, s32[1]{0:T(128)} %bitcast.3.own_ref, bf16[2048,192]{1,0:T(8,128)(2,1)} %get-tuple-element.88.q_ref, ...), custom_call_target="tpu_custom_call" | custom-call | tf_op jit(solution)/shard_map/pallas_call | solution.py:448
  259.7 6.3 %shard_map.230 = (bf16[512,768]{1,0:T(8,128)(2,1)S(1)}, bf16[512,768]{1,0:T(8,128)(2,1)}, f32[8,768]{1,0:T(8,128)S(1)}) custom-call(bf16[1024,192]{1,0:T(8,128)(2,1)S(1)} %get-tuple-element.120.dq_ref.refs_2_, bf16[2048,192]{1,0:T(8,128)(2,1)} %get-tuple-element.115.dk_ref.refs_3_, bf16[2048,192]{1,0:T(8,128)(2,1)} %get-tuple-element.116.dv_ref.refs_4_, ...), custom_call_target="tpu_custom_call" | custom-call | tf_op jit(solution)/shard_map/pallas_call | solution.py:547
  267.0 6.2 %shard_map.229 = (bf16[512,768]{1,0:T(8,128)(2,1)S(1)}, bf16[512,768]{1,0:T(8,128)(2,1)}, f32[8,768]{1,0:T(8,128)S(1)}) custom-call(bf16[1024,192]{1,0:T(8,128)(2,1)S(1)} %get-tuple-element.111.dq_ref.refs_1_, bf16[2048,192]{1,0:T(8,128)(2,1)} %get-tuple-element.115.dk_ref.refs_3_, bf16[2048,192]{1,0:T(8,128)(2,1)} %get-tuple-element.116.dv_ref.refs_4_, ...), custom_call_target="tpu_custom_call" | custom-call | tf_op jit(solution)/shard_map/pallas_call | solution.py:547
  289.8 16.0 %collective-permute-done.56.refs_2_ = bf16[96,1536]{1,0:T(8,128)(2,1)S(1)} collective-permute-done((bf16[96,1536]{1,0:T(8,128)(2,1)}, bf16[96,1536]{1,0:T(8,128)(2,1)S(1)}, u32[]{:S(2)}, u32[]{:S(2)}) %collective-permute-start.56) | collective-permute-done | bytes 294944 | tf_op jit(solution)/shard_map/ppermute | solution.py:36
  306.6 4.6 %shard_map.232 = (bf16[96,192]{1,0:T(8,128)(2,1)S(1)}, bf16[96,192]{1,0:T(8,128)(2,1)S(1)}, bf16[96,192]{1,0:T(8,128)(2,1)S(1)}, bf16[96,192]{1,0:T(8,128)(2,1)S...) custom-call(s32[8]{0:T(128)S(1)} %broadcast_xor_fusion.place_ref, bf16[512,768]{1,0:T(8,128)(2,1)} %copy-done.30, ...), custom_call_target="tpu_custom_call" | custom-call | tf_op jit(solution)/shard_map/pallas_call | solution.py:315
  313.3 6.9 %shard_map.231 = (bf16[96,576]{1,0:T(8,128)(2,1)S(1)}, bf16[96,576]{1,0:T(8,128)(2,1)S(1)}, bf16[96,576]{1,0:T(8,128)(2,1)S(1)}, bf16[96,576]{1,0:T(8,128)(2,1)S...) custom-call(s32[8]{0:T(128)S(1)} %broadcast_xor_fusion.place_ref, ...), custom_call_target="tpu_custom_call" | custom-call | tf_op jit(solution)/shard_map/pallas_call | solution.py:315
  322.4 5.4 %collective-permute-start.45 = (f32[2,768]{1,0:T(2,128)S(1)}, f32[2,768]{1,0:T(2,128)S(1)}, u32[]{:S(2)}, u32[]{:S(2)}) collective-permute-start(f32[2,768]{1,0:T(2,128)S(1)} %add.131), channel_id=1, source_target_pairs={{0,16},{4,20},{8,24},{12,28},{16,0},{20,4},{24,8},{28,12},{1,17},{... | collective-permute-start | bytes 18440 | tf_op jit(solution)/shard_map/ppermute | solution.py:36
  339.4 3.7 %collective-permute-done.50.refs_1_ = bf16[96,768]{1,0:T(8,128)(2,1)S(1)} collective-permute-done((bf16[96,768]{1,0:T(8,128)(2,1)S(1)}, bf16[96,768]{1,0:T(8,128)(2,1)S(1)}, u32[]{:S(2)}, u32[]{:S(2)}) %collective-permute-start.50) | collective-permute-done | bytes 147488 | tf_op jit(solution)/shard_map/ppermute | solution.py:36
  343.1 7.4 %collective-permute-done.51.refs_2_ = bf16[96,768]{1,0:T(8,128)(2,1)S(1)} collective-permute-done((bf16[96,768]{1,0:T(8,128)(2,1)S(1)}, bf16[96,768]{1,0:T(8,128)(2,1)S(1)}, u32[]{:S(2)}, u32[]{:S(2)}) %collective-permute-start.51) | collective-permute-done | bytes 147488 | tf_op jit(solution)/shard_map/ppermute | solution.py:36
  (252 shorter events, 96.3 us)
Async XLA Ops:
  0.6 30.5 %collective-permute-start.5 = (bf16[512,768]{1,0:T(8,128)(2,1)}, bf16[512,768]{1,0:T(8,128)(2,1)}, u32[]{:S(2)}, u32[]{:S(2)}) collective-permute-start(bf16[512,768]{1,0:T(8,128)(2,1)} %xa_ref.1), channel_id=1, source_target_pairs={{0,2},{1,3},{2,0},{3,1},{4,6},{5,7},{6,4},{7,5},{8,10},{9,11},{10,... | collective-permute-start | bytes 2359304 | tf_op jit(solution)/shard_map/ppermute | solution.py:36
  15.6 46.1 %collective-permute-start = (bf16[512,768]{1,0:T(8,128)(2,1)}, bf16[512,768]{1,0:T(8,128)(2,1)}, u32[]{:S(2)}, u32[]{:S(2)}) collective-permute-start(bf16[512,768]{1,0:T(8,128)(2,1)} %xa_ref.1), channel_id=1, source_target_pairs={{0,1},{1,0},{2,3},{3,2},{4,5},{5,4},{6,7},{7,6},{8,9},{9,8},{10,11... | collective-permute-start | bytes 2359304 | tf_op jit(solution)/shard_map/ppermute | solution.py:36
  29.1 33.2 %collective-permute-start.14 = (bf16[512,768]{1,0:T(8,128)(2,1)}, bf16[512,768]{1,0:T(8,128)(2,1)}, u32[]{:S(2)}, u32[]{:S(2)}) collective-permute-start(bf16[512,768]{1,0:T(8,128)(2,1)} %refs_6_), channel_id=1, source_target_pairs={{0,2},{1,3},{2,0},{3,1},{4,6},{5,7},{6,4},{7,5},{8,10},{9,11},{10,... | collective-permute-start | bytes 2359304 | tf_op jit(solution)/shard_map/ppermute | solution.py:36
  31.1 33.3 %collective-permute-start.6 = (bf16[512,768]{1,0:T(8,128)(2,1)}, bf16[512,768]{1,0:T(8,128)(2,1)}, u32[]{:S(2)}, u32[]{:S(2)}) collective-permute-start(bf16[512,768]{1,0:T(8,128)(2,1)} %collective-permute-done.5.refs_2_.refs_0_.xa_ref), channel_id=1, source_target_pairs={{0,1},{1,0},{2,3},{3,2},{4,5},{5,4},{6,7},{7,6},{8,9},{9,8},{10,11... | collective-permute-start | bytes 2359304 | tf_op jit(solution)/shard_map/ppermute | solution.py:36
  47.8 38.7 %collective-permute-start.23 = (bf16[96,1536]{1,0:T(8,128)(2,1)S(1)}, bf16[96,1536]{1,0:T(8,128)(2,1)S(1)}, u32[]{:S(2)}, u32[]{:S(2)}) collective-permute-start(bf16[96,1536]{1,0:T(8,128)(2,1)S(1)} %get-tuple-element.98.refs_13_), channel_id=1, source_target_pairs={{0,16},{4,20},{8,24},{12,28},{16,0},{20,4},{24,8},{28,12},{1,17},{... | collective-permute-start | bytes 884744 | tf_op jit(solution)/shard_map/ppermute | solution.py:36
  49.0 39.1 %collective-permute-start.22 = (bf16[96,1536]{1,0:T(8,128)(2,1)S(1)}, bf16[96,1536]{1,0:T(8,128)(2,1)S(1)}, u32[]{:S(2)}, u32[]{:S(2)}) collective-permute-start(bf16[96,1536]{1,0:T(8,128)(2,1)S(1)} %get-tuple-element.98.refs_13_), channel_id=1, source_target_pairs={{0,8},{4,12},{8,0},{12,4},{16,24},{20,28},{24,16},{28,20},{1,9},{5... | collective-permute-start | bytes 884744 | tf_op jit(solution)/shard_map/ppermute | solution.py:36
  61.7 27.0 %collective-permute-start.25 = (bf16[96,1536]{1,0:T(8,128)(2,1)S(1)}, bf16[96,1536]{1,0:T(8,128)(2,1)S(1)}, u32[]{:S(2)}, u32[]{:S(2)}) collective-permute-start(bf16[96,1536]{1,0:T(8,128)(2,1)S(1)} %get-tuple-element.98.refs_13_), channel_id=1, source_target_pairs={{0,4},{4,0},{8,12},{12,8},{16,20},{20,16},{24,28},{28,24},{1,5},{5... | collective-permute-start | bytes 884744 | tf_op jit(solution)/shard_map/ppermute | solution.py:36
  62.3 27.8 %collective-permute-start.28 = (bf16[96,1536]{1,0:T(8,128)(2,1)S(1)}, bf16[96,1536]{1,0:T(8,128)(2,1)S(1)}, u32[]{:S(2)}, u32[]{:S(2)}) collective-permute-start(bf16[96,1536]{1,0:T(8,128)(2,1)S(1)} %collective-permute-done.24.refs_16_), channel_id=1, source_target_pairs={{0,4},{4,0},{8,12},{12,8},{16,20},{20,16},{24,28},{28,24},{1,5},{5... | collective-permute-start | bytes 884744 | tf_op jit(solution)/shard_map/ppermute | solution.py:36
  64.4 44.9 %collective-permute-start.18 = (bf16[512,768]{1,0:T(8,128)(2,1)}, bf16[512,768]{1,0:T(8,128)(2,1)S(1)}, u32[]{:S(2)}, u32[]{:S(2)}) collective-permute-start(bf16[512,768]{1,0:T(8,128)(2,1)} %collective-permute-done.14.refs_2_.refs_8_), channel_id=1, source_target_pairs={{0,1},{1,0},{2,3},{3,2},{4,5},{5,4},{6,7},{7,6},{8,9},{9,8},{10,11... | collective-permute-start | bytes 2359304 | tf_op jit(solution)/shard_map/ppermute | solution.py:36
  109.4 21.3 %collective-permute-start.4 = (bf16[512,768]{1,0:T(8,128)(2,1)S(1)}, bf16[512,768]{1,0:T(8,128)(2,1)S(1)}, u32[]{:S(2)}, u32[]{:S(2)}) collective-permute-start(bf16[512,768]{1,0:T(8,128)(2,1)S(1)} %copy-done.31), channel_id=1, source_target_pairs={{0,1},{1,0},{2,3},{3,2},{4,5},{5,4},{6,7},{7,6},{8,9},{9,8},{10,11... | collective-permute-start | bytes 2359304 | tf_op jit(solution)/shard_map/ppermute | solution.py:36
  109.9 20.6 %collective-permute-start.12 = (bf16[1024,192]{1,0:T(8,128)(2,1)S(1)}, bf16[1024,192]{1,0:T(8,128)(2,1)S(1)}, u32[]{:S(2)}, u32[]{:S(2)}) collective-permute-start(bf16[1024,192]{1,0:T(8,128)(2,1)S(1)} %get-tuple-element.92.refs_4_.o_ref.refs_5_), channel_id=1, source_target_pairs={{0,2},{1,3},{2,0},{3,1},{4,6},{5,7},{6,4},{7,5},{8,10},{9,11},{10,... | collective-permute-start | bytes 1179656 | tf_op jit(solution)/shard_map/ppermute | solution.py:36
  129.9 25.2 %collective-permute-start.32 = (bf16[512,768]{1,0:T(8,128)(2,1)}, bf16[512,768]{1,0:T(8,128)(2,1)S(1)}, u32[]{:S(2)}, u32[]{:S(2)}) collective-permute-start(bf16[512,768]{1,0:T(8,128)(2,1)} %get-tuple-element.108), channel_id=1, source_target_pairs={{0,1},{1,0},{2,3},{3,2},{4,5},{5,4},{6,7},{7,6},{8,9},{9,8},{10,11... | collective-permute-start | bytes 2359304 | tf_op jit(solution)/shard_map/ppermute | solution.py:36
  179.2 33.4 %collective-permute-start.36 = (bf16[512,768]{1,0:T(8,128)(2,1)S(1)}, bf16[512,768]{1,0:T(8,128)(2,1)S(1)}, u32[]{:S(2)}, u32[]{:S(2)}) collective-permute-start(bf16[512,768]{1,0:T(8,128)(2,1)S(1)} %get-tuple-element.163.ga_ref.refs_0_), channel_id=1, source_target_pairs={{0,1},{1,0},{2,3},{3,2},{4,5},{5,4},{6,7},{7,6},{8,9},{9,8},{10,11... | collective-permute-start | bytes 2359304 | tf_op jit(solution)/shard_map/ppermute | solution.py:36
  197.2 38.2 %collective-permute-start.37 = (bf16[512,768]{1,0:T(8,128)(2,1)S(1)}, bf16[512,768]{1,0:T(8,128)(2,1)S(1)}, u32[]{:S(2)}, u32[]{:S(2)}) collective-permute-start(bf16[512,768]{1,0:T(8,128)(2,1)S(1)} %collective-permute-done.34.ga_ref.refs_2_), channel_id=1, source_target_pairs={{0,1},{1,0},{2,3},{3,2},{4,5},{5,4},{6,7},{7,6},{8,9},{9,8},{10,11... | collective-permute-start | bytes 2359304 | tf_op jit(solution)/shard_map/ppermute | solution.py:36
  197.2 76.2 %collective-permute-start.30 = (bf16[512,768]{1,0:T(8,128)(2,1)}, bf16[512,768]{1,0:T(8,128)(2,1)}, u32[]{:S(2)}, u32[]{:S(2)}) collective-permute-start(bf16[512,768]{1,0:T(8,128)(2,1)} %get-tuple-element.104), channel_id=1, source_target_pairs={{0,1},{1,0},{2,3},{3,2},{4,5},{5,4},{6,7},{7,6},{8,9},{9,8},{10,11... | collective-permute-start | bytes 2359304 | tf_op jit(solution)/shard_map/ppermute | solution.py:36
  210.2 66.5 %collective-permute-start.54 = (bf16[288,1536]{1,0:T(8,128)(2,1)}, bf16[288,1536]{1,0:T(8,128)(2,1)S(1)}, u32[]{:S(2)}, u32[]{:S(2)}) collective-permute-start(bf16[288,1536]{1,0:T(8,128)(2,1)} %get-tuple-element.155), channel_id=1, source_target_pairs={{0,4},{4,0},{8,12},{12,8},{16,20},{20,16},{24,28},{28,24},{1,5},{5... | collective-permute-start | bytes 2654216 | tf_op jit(solution)/shard_map/ppermute | solution.py:36
  211.1 74.1 %collective-permute-start.53 = (bf16[96,1536]{1,0:T(8,128)(2,1)S(1)}, bf16[96,1536]{1,0:T(8,128)(2,1)}, u32[]{:S(2)}, u32[]{:S(2)}) collective-permute-start(bf16[96,1536]{1,0:T(8,128)(2,1)S(1)} %get-tuple-element.153), channel_id=1, source_target_pairs={{0,4},{4,0},{8,12},{12,8},{16,20},{20,16},{24,28},{28,24},{1,5},{5... | collective-permute-start | bytes 884744 | tf_op jit(solution)/shard_map/ppermute | solution.py:36
  212.6 108.5 %collective-permute-start.29 = (bf16[512,768]{1,0:T(8,128)(2,1)}, bf16[512,768]{1,0:T(8,128)(2,1)}, u32[]{:S(2)}, u32[]{:S(2)}) collective-permute-start(bf16[512,768]{1,0:T(8,128)(2,1)} %get-tuple-element.102), channel_id=1, source_target_pairs={{0,1},{1,0},{2,3},{3,2},{4,5},{5,4},{6,7},{7,6},{8,9},{9,8},{10,11... | collective-permute-start | bytes 2359304 | tf_op jit(solution)/shard_map/ppermute | solution.py:36
  277.8 44.6 %collective-permute-start.35 = (bf16[512,768]{1,0:T(8,128)(2,1)}, bf16[512,768]{1,0:T(8,128)(2,1)}, u32[]{:S(2)}, u32[]{:S(2)}) collective-permute-start(bf16[512,768]{1,0:T(8,128)(2,1)} %convert_add_fusion), channel_id=1, source_target_pairs={{0,2},{1,3},{2,0},{3,1},{4,6},{5,7},{6,4},{7,5},{8,10},{9,11},{10,... | collective-permute-start | bytes 2359304 | tf_op jit(solution)/shard_map/ppermute | solution.py:36
  283.2 22.6 %collective-permute-start.56 = (bf16[96,1536]{1,0:T(8,128)(2,1)}, bf16[96,1536]{1,0:T(8,128)(2,1)S(1)}, u32[]{:S(2)}, u32[]{:S(2)}) collective-permute-start(bf16[96,1536]{1,0:T(8,128)(2,1)} %get-tuple-element.166), channel_id=1, source_target_pairs={{0,16},{4,20},{8,24},{12,28},{16,0},{20,4},{24,8},{28,12},{1,17},{... | collective-permute-start | bytes 884744 | tf_op jit(solution)/shard_map/ppermute | solution.py:36
  285.2 20.5 %collective-permute-start.55 = (bf16[96,1536]{1,0:T(8,128)(2,1)S(1)}, bf16[96,1536]{1,0:T(8,128)(2,1)S(1)}, u32[]{:S(2)}, u32[]{:S(2)}) collective-permute-start(bf16[96,1536]{1,0:T(8,128)(2,1)S(1)} %get-tuple-element.167), channel_id=1, source_target_pairs={{0,24},{4,28},{8,16},{12,20},{16,8},{20,12},{24,0},{28,4},{1,25},{... | collective-permute-start | bytes 884744 | tf_op jit(solution)/shard_map/ppermute | solution.py:36
  288.7 31.5 %collective-permute-start.44 = (f32[2,768]{1,0:T(2,128)S(1)}, f32[2,768]{1,0:T(2,128)S(1)}, u32[]{:S(2)}, u32[]{:S(2)}) collective-permute-start(f32[2,768]{1,0:T(2,128)S(1)} %add.130), channel_id=1, source_target_pairs={{0,8},{4,12},{8,0},{12,4},{16,24},{20,28},{24,16},{28,20},{1,9},{5... | collective-permute-start | bytes 18440 | tf_op jit(solution)/shard_map/ppermute | solution.py:36
  311.2 20.1 %collective-permute-start.47 = (bf16[96,192]{1,0:T(8,128)(2,1)S(1)}, bf16[96,192]{1,0:T(8,128)(2,1)S(1)}, u32[]{:S(2)}, u32[]{:S(2)}) collective-permute-start(bf16[96,192]{1,0:T(8,128)(2,1)S(1)} %get-tuple-element.131), channel_id=1, source_target_pairs={{0,4},{4,0},{8,12},{12,8},{16,20},{20,16},{24,28},{28,24},{1,5},{5... | collective-permute-start | bytes 110600 | tf_op jit(solution)/shard_map/ppermute | solution.py:36
  331.3 20.0 %collective-permute-start.38 = (bf16[512,768]{1,0:T(8,128)(2,1)S(1)}, bf16[512,768]{1,0:T(8,128)(2,1)S(1)}, u32[]{:S(2)}, u32[]{:S(2)}) collective-permute-start(bf16[512,768]{1,0:T(8,128)(2,1)S(1)} %copy-done.52), channel_id=1, source_target_pairs={{0,1},{1,0},{2,3},{3,2},{4,5},{5,4},{6,7},{7,6},{8,9},{9,8},{10,11... | collective-permute-start | bytes 2359304 | tf_op jit(solution)/shard_map/ppermute | solution.py:36
  (88 other events, 779.4 us)
where the time goes:
time: 357 us; the launch traced here: 356 us
  Pallas kernels  154 us (43%)
  waiting for transfers between devices  102 us (29%)
  starting transfers between devices  66.7 us (19%)
  local copies, waits for them, and re-layouts  16.7 us (5%)
  other arithmetic  15.5 us (4%)
    ppermute x58, waiting for transfers between devices, swap(): return lax.ppermute(values, axis, [(i, i ^ bits) for i in range(size)])  102 us
    ppermute x58, starting transfers between devices, swap(): return lax.ppermute(values, axis, [(i, i ^ bits) for i in range(size)])  66.7 us
    pallas_call x2, Pallas kernels, attention_backward(): call(functools.partial(backward_kernel, first=first, block=block, heads=h...  45.3 us
    pallas_call x2, Pallas kernels, mlp(): call(functools.partial(mlp_kernel, width=width, heads_width=heads_width,...  34.5 us
    pallas_call x2, Pallas kernels, attention_forward(): call(functools.partial(forward_kernel, first=first, block=block, heads=he...  26.8 us
    pallas_call x3, Pallas kernels, grad_pieces(): call(functools.partial(grads_kernel, groups=counts, steps=tokens // block...  23.9 us
    unnamed x108, local copies, waits for them, and re-layouts  16.2 us
    pallas_call x2, Pallas kernels, rows_back(): call(functools.partial(rows_kernel, width=width, steps=steps), (steps,),...  12.6 us
  transfers between devices with their start and end apart: 58, of which 21 were waited for; matrix products, arithmetic and copies ran while one was open for 3% of the time, Pallas kernels for 43%

commit v1 on v0

--- a/solution.py
+++ b/solution.py
@@ -40,9 +40,10 @@
     return lax.optimization_barrier((values, *earlier))[0]
 
 
-def gather_rows(own):
+def gather_rows(own, ready=()):
     across = swap(own, "narrow", 2)
-    return own, swap(own, "narrow", 1), across, swap(across, "narrow", 1)
+    near, far = after(own, *ready), after(across, *ready)
+    return own, swap(near, "narrow", 1), across, swap(far, "narrow", 1)
 
 
 def pair_sum(parts):
@@ -100,13 +101,13 @@
 
 
 def sum_all(values):
+    values = values + swap(values, "narrow", 2)
     values = values + swap(values, "narrow", 1)
-    values = values + swap(values, "narrow", 2)
     size = lax.axis_size("wide")
     if size != 8:
         values = lax.psum(values, "wide")
     else:
-        for bits in (1, 2, 4):
+        for bits in (2, 4, 1):
             values = values + swap(values, "wide", bits)
     rows = values.shape[1] // size
     return lax.dynamic_slice_in_dim(values, lax.axis_index("wide") * rows, rows, 1)
@@ -145,10 +146,6 @@
     return lax.rsqrt(jnp.mean(values * values, axis=-1, keepdims=True) + EPSILON)
 
 
-def eight(values):
-    return jnp.sum(values.reshape(values.shape[0] // 8, 8, values.shape[1]), axis=0)
-
-
 def parts_in(parts, block):
     per = parts[0].shape[0] // block
     width = parts[0].shape[1]
@@ -190,7 +187,14 @@
     )
 
 
-def pack_kernel(q_ref, k_ref, v_ref, o_ref, g1_ref, g2_ref, gate_ref, up_ref, down_ref, a_ref, b_ref):
+def pack_kernel(*refs):
+    sources, (a_ref, b_ref), held, done = refs[:9], refs[9:11], refs[11:20], refs[20]
+    copies = [pltpu.make_async_copy(src, dst, done.at[j]) for j, (src, dst) in enumerate(zip(sources, held))]
+    for copy in copies:
+        copy.start()
+    for copy in copies:
+        copy.wait()
+    q_ref, k_ref, v_ref, o_ref, g1_ref, g2_ref, gate_ref, up_ref, down_ref = held
     rows, width = q_ref.shape
     hidden = gate_ref.shape[1]
     one = eye(rows)
@@ -220,9 +224,10 @@
     return call(
         pack_kernel,
         (1,),
-        [whole(*arg.shape) for arg in args],
+        [pl.BlockSpec(memory_space=pltpu.HBM)] * len(args),
         [whole(rows, first), whole(rows, second)],
         [shaped((rows, first)), shaped((rows, second))],
+        scratch=[pltpu.VMEM(arg.shape, arg.dtype) for arg in args] + [pltpu.SemaphoreType.DMA((len(args),))],
     )(*args)
 
 
@@ -264,7 +269,10 @@
     )(place, *rows, *pieces)
 
 
-def grads_kernel(place_ref, *refs, groups, steps):
+def grads_kernel(place_ref, *refs, groups, steps, gain):
+    if gain is not None:
+        w_ref, gain_ref, norm_ref = refs[0], refs[1], refs[-2]
+        refs = refs[2:-2] + refs[-1:]
     kept, (far, fourth), total = refs[-7:-3], refs[-3:-1], refs[-1]
     refs = list(refs[:-7])
     step = pl.program_id(0)
@@ -299,10 +307,18 @@
         for j in range(3):
             far[j * rows : (j + 1) * rows, :] = piece(7 - j)
         fourth[...] = piece(4)
-
-
-def grad_pieces(place, groups, block=512):
+        if gain is not None:
+            row, width = gain
+            column = jnp.sum(wide32(w_ref[:, :width]) * total[:, :width], axis=1, keepdims=True)
+            turned = jnp.broadcast_to(column, (column.shape[0], 128)).T
+            norm_ref[...] = turned[:8] / gain_ref[row : row + 1, :]
+
+
+def grad_pieces(place, groups, norm=None, block=512):
     arrays, counts, specs, full = [], [], [], 0
+    if norm:
+        arrays += norm[:2]
+        specs += [whole(*array.shape) for array in norm[:2]]
     for lhs, rhs in groups:
         counts.append((len(lhs), [len(parts) for parts in rhs]))
         for parts in [lhs] + rhs:
@@ -313,15 +329,15 @@
     d = groups[0][0][0].shape[1]
     shapes = [(d // 8, full)] * 4 + [(3 * d // 8, full), (d // 8, full)]
     found = call(
-        functools.partial(grads_kernel, groups=counts, steps=tokens // block),
+        functools.partial(grads_kernel, groups=counts, steps=tokens // block, gain=norm[2:] if norm else None),
         (tokens // block,),
         specs,
-        [whole(*shape) for shape in shapes],
-        [shaped(shape) for shape in shapes],
+        [whole(*shape) for shape in shapes] + [whole(8, d)] * bool(norm),
+        [shaped(shape) for shape in shapes] + [shaped((8, d), jnp.float32)] * bool(norm),
         scratch=[pltpu.VMEM((d, full), jnp.float32)],
         prefetch=1,
     )(place, *arrays)
-    return list(found[:4]), list(found[4:])
+    return list(found[:4]), list(found[4:6]), *found[6:]
 
 
 def finish_kernel(*refs, widths):
@@ -459,8 +475,8 @@
 def mlp_kernel(place_ref, *refs, width, heads_width, steps, near):
     xs, gs, os, ws, gain_ref = refs[:2], refs[2:4], refs[4:8], refs[8:12], refs[12]
     pieces, outs = (refs[13:14], refs[14:]) if near else (refs[13:21], refs[21:])
-    ys, dhs, (h_ref, hid_ref, dg_ref, du_ref, norm_ref) = outs[:2], outs[2:4], outs[4:9]
-    w_ref = pieces[0] if near else outs[9]
+    ys, dhs, (h_ref, hid_ref, dg_ref, du_ref) = outs[:2], outs[2:4], outs[4:8]
+    w_ref = pieces[0] if near else outs[8]
     if not near:
 
         @pl.when(pl.program_id(0) == 0)
@@ -474,7 +490,7 @@
 
         @pl.when(pl.program_id(0) < steps // 2)
         def _():
-            outs[9][...] = m
+            outs[8][...] = m
 
     n = m * inverse_rms(m)
     h = low(n * gain_ref[1:2, :])
@@ -498,12 +514,6 @@
     dh = dot(dgate, w_ref[:, :width], NT) + dot(dup, w_ref[:, width : 2 * width], NT)
     put(dhs, low(dh), steps)
 
-    @pl.when(pl.program_id(0) == 0)
-    def _():
-        norm_ref[...] = jnp.zeros_like(norm_ref)
-
-    norm_ref[...] += eight(dh * n)
-
 
 def mlp(place, xs, gs, os, out_ws, gains, weight, near, block=256):
     part, d = xs[0].shape
@@ -517,41 +527,33 @@
         (steps,),
         parts_in(xs, block) + parts_in(gs, block) + [by_row(block, heads_width), other] * 2
         + [whole(*out_ws[0].shape)] * 4 + [whole(8, d)] + [whole(*piece.shape) for piece in weight],
-        split * 2 + [wide_row] + [thin_row] * 3 + [whole(8, d)] + (split[:1] if near else [whole(d, 3 * width)]),
+        split * 2 + [wide_row] + [thin_row] * 3 + (split[:1] if near else [whole(d, 3 * width)]),
         [shaped((part, d))] * 4 + [shaped((rows, d))] + [shaped((rows, width))] * 3
-        + [shaped((8, d), jnp.float32)] + [shaped((part, d), jnp.float32) if near else shaped((d, 3 * width))],
+        + [shaped((part, d), jnp.float32) if near else shaped((d, 3 * width))],
         prefetch=1,
     )(place, *xs, *gs, *os, *out_ws, gains, *weight)
     return (out[:2], out[2:4]) + tuple(out[4:])
 
 
-def rows_kernel(dq_ref, dk_ref, dv_ref, xa_ref, xb_ref, w_ref, dha_ref, dhb_ref, norm_ref, *, width, steps):
+def rows_kernel(dq_ref, dk_ref, dv_ref, w_ref, dha_ref, dhb_ref, *, width, steps):
     dh = dot(dq_ref[...], w_ref[:, :width], NT)
     dh += dot(dk_ref[...], w_ref[:, width : 2 * width], NT)
     dh += dot(dv_ref[...], w_ref[:, 2 * width : 3 * width], NT)
     put((dha_ref, dhb_ref), low(dh), steps)
-    x = wide32(pick((xa_ref, xb_ref), steps))
-
-    @pl.when(pl.program_id(0) == 0)
-    def _():
-        norm_ref[...] = jnp.zeros_like(norm_ref)
-
-    norm_ref[...] += eight(dh * x * inverse_rms(x))
-
-
-def rows_back(dq, dk, dv, xs, weight, first, block=256):
+
+
+def rows_back(dq, dk, dv, weight, first, block=512):
     count, width = dq.shape
-    part, d = xs[0].shape
+    d = weight.shape[0]
     at, steps = first // block, count // block
     late = pl.BlockSpec((block, width), lambda i, *_: (i + at, 0))
-    dha, dhb, norm = call(
+    return call(
         functools.partial(rows_kernel, width=width, steps=steps),
         (steps,),
-        [by_row(block, width), late, late] + parts_in(xs, block) + [whole(*weight.shape)],
-        halves(block, d, steps) + [whole(8, d)],
-        [shaped((part, d))] * 2 + [shaped((8, d), jnp.float32)],
-    )(dq, dk, dv, *xs, weight)
-    return (dha, dhb), norm
+        [by_row(block, width), late, late, whole(*weight.shape)],
+        halves(block, d, steps),
+        [shaped((count // 2, d))] * 2,
+    )(dq, dk, dv, weight)
 
 
 def norm_back(values, gain, grad):
@@ -573,8 +575,8 @@
         query_weight, key_weight, value_weight, out_weight, norm1_gain, norm2_gain,
         gate_weight, up_weight, down_weight.T,
     )
-    x = gather_rows(patches)
     attn_pieces = gather_wide(attn_own)
+    x = gather_rows(patches, attn_pieces[2:3])
     mlp_pieces = gather_wide(after(mlp_own, *attn_pieces[1:4]), attn_pieces[4:])
     g = gather_rows(after(cotangent, *attn_pieces[1:4]))
 
@@ -588,41 +590,43 @@
     o_near_across = swap(o_far, "narrow", 2)
     o_far_all = (o_far, swap(o_far, "narrow", 1)) + o_far_across
     o_near_all = (o_near, swap(o_near, "narrow", 1), o_near_across, swap(o_near_across, "narrow", 1))
-    y_far, dh_far, h2_far, hid_far, dg_far, du_far, n2_far, mlp_w = mlp(
+    y_far, dh_far, h2_far, hid_far, dg_far, du_far, mlp_w = mlp(
         place, x[2:], g[2:], o_far_all, out_ws, gains, mlp_pieces, False
     )
     from_far = cross(pair_sum(dh_far))
-    y_near, dh_near, h2_near, hid_near, dg_near, du_near, n2_near, middle_own = mlp(
+    y_near, dh_near, h2_near, hid_near, dg_near, du_near, middle_own = mlp(
         place, x[:2], g[:2], o_near_all, out_ws, gains, [mlp_w], True
     )
     gain_one, gain_two = gains[0:1], gains[1:2]
     dh_two = pair_sum(dh_near) + from_far
-    mlp_parts = grad_pieces(
+    mlp_kept, mlp_sent, norm_two = grad_pieces(
         place,
         [([h2_near, h2_far], [[dg_near, dg_far], [du_near, du_far]]), (list(g), [[hid_near, hid_far]])],
-    )
-    mlp_sent = send_x(mlp_parts[1])
+        [mlp_w, gains, 1, 2 * hidden],
+    )
+    mlp_sent = send_x(mlp_sent)
     middle_grad_own = wide32(cotangent) + norm_back(middle_own, gain_two, dh_two)
     d = gather_rows(low(middle_grad_own))
-    grad_gate, grad_up, grad_down = finish(reduce_wide([(mlp_parts[0], mlp_sent)]), (hidden, hidden, hidden), False)
+    mlp_pieces = reduce_wide([(mlp_kept, mlp_sent)])
+    grad_gate, grad_up, grad_down = finish(mlp_pieces, (hidden, hidden, hidden), False)
     dq_near, dk_sum, dv_sum = attention_backward(scalars, q, k, v, d[:2], out_w, o_near, lse_near, ())
     output = low(middle_own + pair_sum(y_near) + cross(after(pair_sum(y_far), d[2])))
-    out_parts = grad_pieces(place, [(list(d), [[o_near, o_far]])])
-    out_sent = send_x(out_parts[1])
+    out_kept, out_sent = grad_pieces(place, [(list(d), [[o_near, o_far]])])
+    out_sent = send_x(out_sent)
     dq_far, dk, dv = attention_backward(scalars, q, k, v, d[2:], out_w, o_far, lse_far, (dk_sum, dv_sum))
-    attn_parts = grad_pieces(place, [([h_one], [[dq_near, dq_far], [dk], [dv]])])
-    attn_sent = send_x(attn_parts[1])
-    dh_far, n1_far = rows_back(dq_far, dk, dv, x[2:], qkv_w, half)
+    attn_kept, attn_sent, norm_one = grad_pieces(
+        place, [([h_one], [[dq_near, dq_far], [dk], [dv]])], [qkv_w, gains, 0, 3 * width]
+    )
+    attn_sent = send_x(attn_sent)
+    norms = sum_all(jnp.concatenate([norm_one[:1], norm_two[:1]], axis=0))
+    dh_far = rows_back(dq_far, dk, dv, qkv_w, half)
     from_far = cross(pair_sum(dh_far))
-    dh_near, n1_near = rows_back(dq_near, dk, dv, x[:2], qkv_w, 0)
+    dh_near = rows_back(dq_near, dk, dv, qkv_w, 0)
     grad_query, grad_key, grad_value, grad_out = finish(
-        reduce_wide([(attn_parts[0], attn_sent), (out_parts[0], out_sent)]), (width, width, width, width), True
+        reduce_wide([(attn_kept, attn_sent), (out_kept, out_sent)]), (width, width, width, width), True
     )
     dh_one = pair_sum(dh_near) + from_far
     grad_input = middle_grad_own + norm_back(wide32(patches), gain_one, dh_one)
-    norms = sum_all(
-        jnp.stack([jnp.sum(n1_near + n1_far, axis=0), jnp.sum(n2_near + n2_far, axis=0)], axis=0)
-    )
     return (
         output, grad_input, norms[0], grad_query, grad_key, grad_value, grad_out, norms[1],
         grad_gate, grad_up, grad_down.T,

time: 357 us -> 368 us (1.031)
  waiting for transfers between devices: 102 us -> 120 us
  starting transfers between devices: 66.7 us -> 63 us
    ppermute x58, waiting for transfers between devices: 102 us -> 120 us  [swap(): return lax.ppermute(values, axis, [(i, i ^ bits) for i in range(size)])]
    pallas_call x2, Pallas kernels: 12.6 us -> 8.67 us  [rows_back(): call(functools.partial(rows_kernel, width=width, steps=steps), (steps,),...]
    ppermute x58, starting transfers between devices: 66.7 us -> 63 us  [swap(): return lax.ppermute(values, axis, [(i, i ^ bits) for i in range(size)])]
    unnamed x108 -> x104, local copies, waits for them, and re-layouts: 16.2 us -> 16.5 us
  transfers between devices with their start and end apart: 58 -> 58, of which waited for: 21 -> 21; matrix products, arithmetic and copies ran while one was open for 3% -> 3% of each run, Pallas kernels for 43% -> 41%
where the time goes in v1:
time: 368 us; the launch traced here: 367 us
  Pallas kernels  152 us (41%)
  waiting for transfers between devices  120 us (33%)
  starting transfers between devices  63 us (17%)
  local copies, waits for them, and re-layouts  17 us (5%)
  other arithmetic  14.2 us (4%)
    ppermute x58, waiting for transfers between devices, swap(): return lax.ppermute(values, axis, [(i, i ^ bits) for i in range(size)])  120 us
    ppermute x58, starting transfers between devices, swap(): return lax.ppermute(values, axis, [(i, i ^ bits) for i in range(size)])  63 us
    pallas_call x2, Pallas kernels, attention_backward(): call(functools.partial(backward_kernel, first=first, block=block, heads=h...  45.3 us
    pallas_call x2, Pallas kernels, mlp(): call(functools.partial(mlp_kernel, width=width, heads_width=heads_width,...  33.9 us
    pallas_call x2, Pallas kernels, attention_forward(): call(functools.partial(forward_kernel, first=first, block=block, heads=he...  26.8 us
    pallas_call x3, Pallas kernels, grad_pieces(): call(functools.partial(grads_kernel, groups=counts, steps=tokens // block...  25.8 us
    unnamed x104, local copies, waits for them, and re-layouts  16.5 us
    pallas_call x2, Pallas kernels, rows_back(): call(functools.partial(rows_kernel, width=width, steps=steps), (steps,),...  8.67 us
  transfers between devices with their start and end apart: 58, of which 21 were waited for; matrix products, arithmetic and copies ran while one was open for 3% of the time, Pallas kernels for 41%

profile of v1, /device:TPU:0, one launch (start us, length us, event | category | flops | bytes accessed | tf_op | source)
XLA Modules:
  0.0 366.9 jit_solution(7097254833671033428)
XLA Ops:
  16.1 11.1 %collective-permute-done.refs_6_ = bf16[96,896]{1,0:T(8,128)(2,1)S(1)} collective-permute-done((bf16[96,896]{1,0:T(8,128)(2,1)S(1)}, bf16[96,896]{1,0:T(8,128)(2,1)S(1)}, u32[]{:S(2)}, u32[]{:S(2)}) %collective-permute-start) | collective-permute-done | bytes 172064 | tf_op jit(solution)/shard_map/ppermute | solution.py:36
  29.9 5.2 %collective-permute-done.7.refs_8_ = bf16[96,896]{1,0:T(8,128)(2,1)S(1)} collective-permute-done((bf16[96,896]{1,0:T(8,128)(2,1)S(1)}, bf16[96,896]{1,0:T(8,128)(2,1)S(1)}, u32[]{:S(2)}, u32[]{:S(2)}) %collective-permute-start.7) | collective-permute-done | bytes 172064 | tf_op jit(solution)/shard_map/ppermute | solution.py:36
  47.2 4.5 %collective-permute-start.23 = (bf16[96,1536]{1,0:T(8,128)(2,1)S(1)}, bf16[96,1536]{1,0:T(8,128)(2,1)S(1)}, u32[]{:S(2)}, u32[]{:S(2)}) collective-permute-start(bf16[96,1536]{1,0:T(8,128)(2,1)S(1)} %get-tuple-element.100.refs_13_), channel_id=1, source_target_pairs={{0,16},{4,20},{8,24},{12,28},{16,0},{20,4},{24,8},{28,12},{1,17},{... | collective-permute-start | bytes 884744 | tf_op jit(solution)/shard_map/ppermute | solution.py:36
  51.7 9.5 %collective-permute-start.22 = (bf16[96,1536]{1,0:T(8,128)(2,1)S(1)}, bf16[96,1536]{1,0:T(8,128)(2,1)S(1)}, u32[]{:S(2)}, u32[]{:S(2)}) collective-permute-start(bf16[96,1536]{1,0:T(8,128)(2,1)S(1)} %get-tuple-element.100.refs_13_), channel_id=1, source_target_pairs={{0,8},{4,12},{8,0},{12,4},{16,24},{20,28},{24,16},{28,20},{1,9},{5... | collective-permute-start | bytes 884744 | tf_op jit(solution)/shard_map/ppermute | solution.py:36
  63.9 8.6 %shard_map.222 = (bf16[2048,768]{1,0:T(8,128)(2,1)}, bf16[2048,192]{1,0:T(8,128)(2,1)}, bf16[2048,192]{1,0:T(8,128)(2,1)}, bf16[2048,192]{1,0:T(8,128)(2,1)}, bf...) custom-call(s32[8]{0:T(128)S(1)} %broadcast_xor_fusion.place_ref, ...), custom_call_target="tpu_custom_call" | custom-call | tf_op jit(solution)/shard_map/pallas_call | solution.py:262
  72.6 13.4 %shard_map.223 = (bf16[1024,192]{1,0:T(8,128)(2,1)S(1)}, f32[1024,3]{1,0:T(8,128)S(1)}) custom-call(s32[1,4]{1,0:T(1,128)S(1)} %copy-done.21, s32[1,4]{1,0:T(1,128)S(1)} %copy-done.22, s32[1]{0:T(128)} %bitcast.3.own_ref, bf16[2048,192]{1,0:T(8,128)(2,1)} %get-tuple-element.90.q_ref, bf16[2048,192]{1,0:T(8,128)(2,1)} %get-tuple-element.91.k_ref, ...), custom_call_target="tpu_custom_call" | custom-call | tf_op jit(solution)/shard_map/pallas_call | solution.py:409
  90.2 13.4 %shard_map.224 = (bf16[1024,192]{1,0:T(8,128)(2,1)S(1)}, f32[1024,3]{1,0:T(8,128)S(1)}) custom-call(s32[1,4]{1,0:T(1,128)S(1)} %copy-done.21, s32[1,4]{1,0:T(1,128)S(1)} %copy-done.22, s32[1]{0:T(128)} %bitcast.3.own_ref, bf16[2048,192]{1,0:T(8,128)(2,1)} %get-tuple-element.90.q_ref, bf16[2048,192]{1,0:T(8,128)(2,1)} %get-tuple-element.91.k_ref, ...), custom_call_target="tpu_custom_call" | custom-call | tf_op jit(solution)/shard_map/pallas_call | solution.py:409
  104.2 4.7 %collective-permute-done.16.refs_10_ = bf16[768,192]{1,0:T(8,128)(2,1)S(1)} collective-permute-done((bf16[768,192]{1,0:T(8,128)(2,1)S(1)}, bf16[768,192]{1,0:T(8,128)(2,1)S(1)}, u32[]{:S(2)}, u32[]{:S(2)}) %collective-permute-start.16) | collective-permute-done | bytes 294944 | tf_op jit(solution)/shard_map/ppermute | solution.py:36
  113.3 17.3 %shard_map.225 = (bf16[512,768]{1,0:T(8,128)(2,1)}, bf16[512,768]{1,0:T(8,128)(2,1)}, bf16[512,768]{1,0:T(8,128)(2,1)}, bf16[512,768]{1,0:T(8,128)(2,1)}, bf16[1...) custom-call(s32[8]{0:T(128)S(1)} %broadcast_xor_fusion.place_ref, ...), custom_call_target="tpu_custom_call" | custom-call | tf_op jit(solution)/shard_map/pallas_call | solution.py:525
  138.4 16.7 %shard_map.226 = (bf16[512,768]{1,0:T(8,128)(2,1)}, bf16[512,768]{1,0:T(8,128)(2,1)}, bf16[512,768]{1,0:T(8,128)(2,1)}, bf16[512,768]{1,0:T(8,128)(2,1)}, bf16[1...) custom-call(s32[8]{0:T(128)S(1)} %broadcast_xor_fusion.place_ref, ...), custom_call_target="tpu_custom_call" | custom-call | tf_op jit(solution)/shard_map/pallas_call | solution.py:525
  157.7 17.7 %collective-permute-done.33 = bf16[512,768]{1,0:T(8,128)(2,1)S(1)} collective-permute-done((bf16[512,768]{1,0:T(8,128)(2,1)S(1)}, bf16[512,768]{1,0:T(8,128)(2,1)S(1)}, u32[]{:S(2)}, u32[]{:S(2)}) %collective-permute-start.33) | collective-permute-done | bytes 786464 | tf_op jit(solution)/shard_map/ppermute | solution.py:36
  178.9 18.5 %collective-permute-done.34.ga_ref.refs_2_ = bf16[512,768]{1,0:T(8,128)(2,1)S(1)} collective-permute-done((bf16[512,768]{1,0:T(8,128)(2,1)S(1)}, bf16[512,768]{1,0:T(8,128)(2,1)S(1)}, u32[]{:S(2)}, u32[]{:S(2)}) %collective-permute-start.34) | collective-permute-done | bytes 786464 | tf_op jit(solution)/shard_map/ppermute | solution.py:36
  197.9 13.6 %shard_map.232 = (bf16[96,1536]{1,0:T(8,128)(2,1)S(1)}, bf16[96,1536]{1,0:T(8,128)(2,1)S(1)}, bf16[96,1536]{1,0:T(8,128)(2,1)S(1)}, bf16[96,1536]{1,0:T(8,128)(2...) custom-call(s32[8]{0:T(128)S(1)} %broadcast_xor_fusion.place_ref, ...), custom_call_target="tpu_custom_call" | custom-call | tf_op jit(solution)/shard_map/pallas_call | solution.py:331
  214.8 21.8 %shard_map.227 = (bf16[1024,192]{1,0:T(8,128)(2,1)S(1)}, f32[192,2048]{1,0:T(8,128)}, f32[192,2048]{1,0:T(8,128)}) custom-call(s32[1,4]{1,0:T(1,128)S(1)} %copy-done.21, s32[1,4]{1,0:T(1,128)S(1)} %copy-done.22, s32[1]{0:T(128)} %bitcast.3.own_ref, bf16[2048,192]{1,0:T(8,128)(2,1)} %get-tuple-element.90.q_ref, bf16[2048,192]{1,0:T(8,128)(2,1)} %get-tuple-element.91.k_ref, ...), custom_call_target="tpu_custom_call" | custom-call | tf_op jit(solution)/shard_map/pallas_call | solution.py:464
  237.6 23.4 %shard_map.228 = (bf16[1024,192]{1,0:T(8,128)(2,1)S(1)}, bf16[2048,192]{1,0:T(8,128)(2,1)}, bf16[2048,192]{1,0:T(8,128)(2,1)}) custom-call(s32[1,4]{1,0:T(1,128)S(1)} %copy-done.21, s32[1,4]{1,0:T(1,128)S(1)} %copy-done.22, s32[1]{0:T(128)} %bitcast.3.own_ref, bf16[2048,192]{1,0:T(8,128)(2,1)} %get-tuple-element.90.q_ref, ...), custom_call_target="tpu_custom_call" | custom-call | tf_op jit(solution)/shard_map/pallas_call | solution.py:464
  261.8 7.5 %shard_map.231 = (bf16[96,576]{1,0:T(8,128)(2,1)S(1)}, bf16[96,576]{1,0:T(8,128)(2,1)S(1)}, bf16[96,576]{1,0:T(8,128)(2,1)S(1)}, bf16[96,576]{1,0:T(8,128)(2,1)S...) custom-call(s32[8]{0:T(128)S(1)} %broadcast_xor_fusion.place_ref, ...), custom_call_target="tpu_custom_call" | custom-call | tf_op jit(solution)/shard_map/pallas_call | solution.py:331
  276.9 7.0 %collective-permute-done.43 = f32[2,768]{1,0:T(2,128)S(1)} collective-permute-done((f32[2,768]{1,0:T(2,128)S(1)}, f32[2,768]{1,0:T(2,128)S(1)}, u32[]{:S(2)}, u32[]{:S(2)}) %collective-permute-start.43) | collective-permute-done | bytes 6176 | tf_op jit(solution)/shard_map/ppermute | solution.py:36
  289.8 16.8 %collective-permute-done.56.refs_2_ = bf16[96,1536]{1,0:T(8,128)(2,1)S(1)} collective-permute-done((bf16[96,1536]{1,0:T(8,128)(2,1)}, bf16[96,1536]{1,0:T(8,128)(2,1)S(1)}, u32[]{:S(2)}, u32[]{:S(2)}) %collective-permute-start.56) | collective-permute-done | bytes 294944 | tf_op jit(solution)/shard_map/ppermute | solution.py:36
  307.5 5.4 %collective-permute-done.44 = f32[2,768]{1,0:T(2,128)S(1)} collective-permute-done((f32[2,768]{1,0:T(2,128)S(1)}, f32[2,768]{1,0:T(2,128)S(1)}, u32[]{:S(2)}, u32[]{:S(2)}) %collective-permute-start.44) | collective-permute-done | bytes 6176 | tf_op jit(solution)/shard_map/ppermute | solution.py:36
  317.4 4.3 %shard_map.230 = (bf16[512,768]{1,0:T(8,128)(2,1)S(1)}, bf16[512,768]{1,0:T(8,128)(2,1)}) custom-call(bf16[1024,192]{1,0:T(8,128)(2,1)S(1)} %copy-done.7, bf16[2048,192]{1,0:T(8,128)(2,1)} %get-tuple-element.117.dk_ref.refs_5_, bf16[2048,192]{1,0:T(8,128)(2,1)} %get-tuple-element.118.dv_ref.refs_6_, bf16[768,896]{1,0:T(8,128)(2,1)} %get-tuple-element.119.w_ref.refs_0_), custom_call_target="tpu_custom_call" | custom-call | tf_op jit(solution)/shard_map/pallas_call | solution.py:550
  321.7 4.3 %shard_map.229 = (bf16[512,768]{1,0:T(8,128)(2,1)S(1)}, bf16[512,768]{1,0:T(8,128)(2,1)}) custom-call(bf16[1024,192]{1,0:T(8,128)(2,1)S(1)} %get-tuple-element.113.dq_ref.refs_3_, bf16[2048,192]{1,0:T(8,128)(2,1)} %get-tuple-element.117.dk_ref.refs_5_, bf16[2048,192]{1,0:T(8,128)(2,1)} %get-tuple-element.118.dv_ref.refs_6_, ...), custom_call_target="tpu_custom_call" | custom-call | tf_op jit(solution)/shard_map/pallas_call | solution.py:550
  326.1 4.6 %shard_map.233 = (bf16[96,192]{1,0:T(8,128)(2,1)S(1)}, bf16[96,192]{1,0:T(8,128)(2,1)S(1)}, bf16[96,192]{1,0:T(8,128)(2,1)S(1)}, bf16[96,192]{1,0:T(8,128)(2,1)S...) custom-call(s32[8]{0:T(128)S(1)} %broadcast_xor_fusion.place_ref, bf16[512,768]{1,0:T(8,128)(2,1)} %copy-done.31, ...), custom_call_target="tpu_custom_call" | custom-call | tf_op jit(solution)/shard_map/pallas_call | solution.py:331
  339.4 7.8 %collective-permute-done.48 = bf16[288,576]{1,0:T(8,128)(2,1)S(1)} collective-permute-done((bf16[288,576]{1,0:T(8,128)(2,1)S(1)}, bf16[288,576]{1,0:T(8,128)(2,1)S(1)}, u32[]{:S(2)}, u32[]{:S(2)}) %collective-permute-start.48) | collective-permute-done | bytes 331808 | tf_op jit(solution)/shard_map/ppermute | solution.py:36
  355.9 6.9 %collective-permute-done.51.refs_2_ = bf16[96,768]{1,0:T(8,128)(2,1)S(1)} collective-permute-done((bf16[96,768]{1,0:T(8,128)(2,1)S(1)}, bf16[96,768]{1,0:T(8,128)(2,1)S(1)}, u32[]{:S(2)}, u32[]{:S(2)}) %collective-permute-start.51) | collective-permute-done | bytes 147488 | tf_op jit(solution)/shard_map/ppermute | solution.py:36
  (246 shorter events, 101.6 us)
Async XLA Ops:
  0.6 28.8 %collective-permute-start.5 = (bf16[512,768]{1,0:T(8,128)(2,1)}, bf16[512,768]{1,0:T(8,128)(2,1)}, u32[]{:S(2)}, u32[]{:S(2)}) collective-permute-start(bf16[512,768]{1,0:T(8,128)(2,1)} %refs_0_.5), channel_id=1, source_target_pairs={{0,2},{1,3},{2,0},{3,1},{4,6},{5,7},{6,4},{7,5},{8,10},{9,11},{10,... | collective-permute-start | bytes 2359304 | tf_op jit(solution)/shard_map/ppermute | solution.py:36
  27.2 34.0 %collective-permute-start.1 = (bf16[512,768]{1,0:T(8,128)(2,1)}, bf16[512,768]{1,0:T(8,128)(2,1)}, u32[]{:S(2)}, u32[]{:S(2)}) collective-permute-start(bf16[512,768]{1,0:T(8,128)(2,1)} %refs_0_.5), channel_id=1, source_target_pairs={{0,1},{1,0},{2,3},{3,2},{4,5},{5,4},{6,7},{7,6},{8,9},{9,8},{10,11... | collective-permute-start | bytes 2359304 | tf_op jit(solution)/shard_map/ppermute | solution.py:36
  27.4 35.2 %collective-permute-start.14 = (bf16[512,768]{1,0:T(8,128)(2,1)}, bf16[512,768]{1,0:T(8,128)(2,1)}, u32[]{:S(2)}, u32[]{:S(2)}) collective-permute-start(bf16[512,768]{1,0:T(8,128)(2,1)} %refs_8_), channel_id=1, source_target_pairs={{0,2},{1,3},{2,0},{3,1},{4,6},{5,7},{6,4},{7,5},{8,10},{9,11},{10,... | collective-permute-start | bytes 2359304 | tf_op jit(solution)/shard_map/ppermute | solution.py:36
  29.4 34.4 %collective-permute-start.6 = (bf16[512,768]{1,0:T(8,128)(2,1)}, bf16[512,768]{1,0:T(8,128)(2,1)}, u32[]{:S(2)}, u32[]{:S(2)}) collective-permute-start(bf16[512,768]{1,0:T(8,128)(2,1)} %collective-permute-done.5.refs_2_.refs_0_), channel_id=1, source_target_pairs={{0,1},{1,0},{2,3},{3,2},{4,5},{5,4},{6,7},{7,6},{8,9},{9,8},{10,11... | collective-permute-start | bytes 2359304 | tf_op jit(solution)/shard_map/ppermute | solution.py:36
  47.2 38.9 %collective-permute-start.23 = (bf16[96,1536]{1,0:T(8,128)(2,1)S(1)}, bf16[96,1536]{1,0:T(8,128)(2,1)S(1)}, u32[]{:S(2)}, u32[]{:S(2)}) collective-permute-start(bf16[96,1536]{1,0:T(8,128)(2,1)S(1)} %get-tuple-element.100.refs_13_), channel_id=1, source_target_pairs={{0,16},{4,20},{8,24},{12,28},{16,0},{20,4},{24,8},{28,12},{1,17},{... | collective-permute-start | bytes 884744 | tf_op jit(solution)/shard_map/ppermute | solution.py:36
  51.7 36.0 %collective-permute-start.22 = (bf16[96,1536]{1,0:T(8,128)(2,1)S(1)}, bf16[96,1536]{1,0:T(8,128)(2,1)S(1)}, u32[]{:S(2)}, u32[]{:S(2)}) collective-permute-start(bf16[96,1536]{1,0:T(8,128)(2,1)S(1)} %get-tuple-element.100.refs_13_), channel_id=1, source_target_pairs={{0,8},{4,12},{8,0},{12,4},{16,24},{20,28},{24,16},{28,20},{1,9},{5... | collective-permute-start | bytes 884744 | tf_op jit(solution)/shard_map/ppermute | solution.py:36
  61.2 28.0 %collective-permute-start.25 = (bf16[96,1536]{1,0:T(8,128)(2,1)S(1)}, bf16[96,1536]{1,0:T(8,128)(2,1)S(1)}, u32[]{:S(2)}, u32[]{:S(2)}) collective-permute-start(bf16[96,1536]{1,0:T(8,128)(2,1)S(1)} %get-tuple-element.100.refs_13_), channel_id=1, source_target_pairs={{0,4},{4,0},{8,12},{12,8},{16,20},{20,16},{24,28},{28,24},{1,5},{5... | collective-permute-start | bytes 884744 | tf_op jit(solution)/shard_map/ppermute | solution.py:36
  62.7 27.0 %collective-permute-start.28 = (bf16[96,1536]{1,0:T(8,128)(2,1)S(1)}, bf16[96,1536]{1,0:T(8,128)(2,1)S(1)}, u32[]{:S(2)}, u32[]{:S(2)}) collective-permute-start(bf16[96,1536]{1,0:T(8,128)(2,1)S(1)} %collective-permute-done.24.refs_16_), channel_id=1, source_target_pairs={{0,4},{4,0},{8,12},{12,8},{16,20},{20,16},{24,28},{28,24},{1,5},{5... | collective-permute-start | bytes 884744 | tf_op jit(solution)/shard_map/ppermute | solution.py:36
  63.9 45.5 %collective-permute-start.18 = (bf16[512,768]{1,0:T(8,128)(2,1)}, bf16[512,768]{1,0:T(8,128)(2,1)S(1)}, u32[]{:S(2)}, u32[]{:S(2)}) collective-permute-start(bf16[512,768]{1,0:T(8,128)(2,1)} %collective-permute-done.14.refs_2_.refs_10_), channel_id=1, source_target_pairs={{0,1},{1,0},{2,3},{3,2},{4,5},{5,4},{6,7},{7,6},{8,9},{9,8},{10,11... | collective-permute-start | bytes 2359304 | tf_op jit(solution)/shard_map/ppermute | solution.py:36
  109.4 21.9 %collective-permute-start.4 = (bf16[512,768]{1,0:T(8,128)(2,1)S(1)}, bf16[512,768]{1,0:T(8,128)(2,1)S(1)}, u32[]{:S(2)}, u32[]{:S(2)}) collective-permute-start(bf16[512,768]{1,0:T(8,128)(2,1)S(1)} %copy-done.29), channel_id=1, source_target_pairs={{0,1},{1,0},{2,3},{3,2},{4,5},{5,4},{6,7},{7,6},{8,9},{9,8},{10,11... | collective-permute-start | bytes 2359304 | tf_op jit(solution)/shard_map/ppermute | solution.py:36
  130.5 24.8 %collective-permute-start.32 = (bf16[512,768]{1,0:T(8,128)(2,1)}, bf16[512,768]{1,0:T(8,128)(2,1)S(1)}, u32[]{:S(2)}, u32[]{:S(2)}) collective-permute-start(bf16[512,768]{1,0:T(8,128)(2,1)} %get-tuple-element.110), channel_id=1, source_target_pairs={{0,1},{1,0},{2,3},{3,2},{4,5},{5,4},{6,7},{7,6},{8,9},{9,8},{10,11... | collective-permute-start | bytes 2359304 | tf_op jit(solution)/shard_map/ppermute | solution.py:36
  178.9 35.1 %collective-permute-start.36 = (bf16[512,768]{1,0:T(8,128)(2,1)S(1)}, bf16[512,768]{1,0:T(8,128)(2,1)S(1)}, u32[]{:S(2)}, u32[]{:S(2)}) collective-permute-start(bf16[512,768]{1,0:T(8,128)(2,1)S(1)} %get-tuple-element.163.ga_ref.refs_0_), channel_id=1, source_target_pairs={{0,1},{1,0},{2,3},{3,2},{4,5},{5,4},{6,7},{7,6},{8,9},{9,8},{10,11... | collective-permute-start | bytes 2359304 | tf_op jit(solution)/shard_map/ppermute | solution.py:36
  197.4 39.3 %collective-permute-start.37 = (bf16[512,768]{1,0:T(8,128)(2,1)S(1)}, bf16[512,768]{1,0:T(8,128)(2,1)S(1)}, u32[]{:S(2)}, u32[]{:S(2)}) collective-permute-start(bf16[512,768]{1,0:T(8,128)(2,1)S(1)} %collective-permute-done.34.ga_ref.refs_2_), channel_id=1, source_target_pairs={{0,1},{1,0},{2,3},{3,2},{4,5},{5,4},{6,7},{7,6},{8,9},{9,8},{10,11... | collective-permute-start | bytes 2359304 | tf_op jit(solution)/shard_map/ppermute | solution.py:36
  197.4 72.5 %collective-permute-start.30 = (bf16[512,768]{1,0:T(8,128)(2,1)S(1)}, bf16[512,768]{1,0:T(8,128)(2,1)}, u32[]{:S(2)}, u32[]{:S(2)}) collective-permute-start(bf16[512,768]{1,0:T(8,128)(2,1)S(1)} %copy-done.49), channel_id=1, source_target_pairs={{0,1},{1,0},{2,3},{3,2},{4,5},{5,4},{6,7},{7,6},{8,9},{9,8},{10,11... | collective-permute-start | bytes 2359304 | tf_op jit(solution)/shard_map/ppermute | solution.py:36
  211.6 61.6 %collective-permute-start.54 = (bf16[288,1536]{1,0:T(8,128)(2,1)}, bf16[288,1536]{1,0:T(8,128)(2,1)S(1)}, u32[]{:S(2)}, u32[]{:S(2)}) collective-permute-start(bf16[288,1536]{1,0:T(8,128)(2,1)} %get-tuple-element.155), channel_id=1, source_target_pairs={{0,4},{4,0},{8,12},{12,8},{16,20},{20,16},{24,28},{28,24},{1,5},{5... | collective-permute-start | bytes 2654216 | tf_op jit(solution)/shard_map/ppermute | solution.py:36
  213.4 72.1 %collective-permute-start.53 = (bf16[96,1536]{1,0:T(8,128)(2,1)S(1)}, bf16[96,1536]{1,0:T(8,128)(2,1)}, u32[]{:S(2)}, u32[]{:S(2)}) collective-permute-start(bf16[96,1536]{1,0:T(8,128)(2,1)S(1)} %get-tuple-element.153), channel_id=1, source_target_pairs={{0,4},{4,0},{8,12},{12,8},{16,20},{20,16},{24,28},{28,24},{1,5},{5... | collective-permute-start | bytes 884744 | tf_op jit(solution)/shard_map/ppermute | solution.py:36
  214.0 100.5 %collective-permute-start.29 = (bf16[512,768]{1,0:T(8,128)(2,1)}, bf16[512,768]{1,0:T(8,128)(2,1)}, u32[]{:S(2)}, u32[]{:S(2)}) collective-permute-start(bf16[512,768]{1,0:T(8,128)(2,1)} %get-tuple-element.104), channel_id=1, source_target_pairs={{0,1},{1,0},{2,3},{3,2},{4,5},{5,4},{6,7},{7,6},{8,9},{9,8},{10,11... | collective-permute-start | bytes 2359304 | tf_op jit(solution)/shard_map/ppermute | solution.py:36
  274.2 40.2 %collective-permute-start.35 = (bf16[512,768]{1,0:T(8,128)(2,1)}, bf16[512,768]{1,0:T(8,128)(2,1)}, u32[]{:S(2)}, u32[]{:S(2)}) collective-permute-start(bf16[512,768]{1,0:T(8,128)(2,1)} %convert_add_fusion), channel_id=1, source_target_pairs={{0,2},{1,3},{2,0},{3,1},{4,6},{5,7},{6,4},{7,5},{8,10},{9,11},{10,... | collective-permute-start | bytes 2359304 | tf_op jit(solution)/shard_map/ppermute | solution.py:36
  283.9 22.7 %collective-permute-start.56 = (bf16[96,1536]{1,0:T(8,128)(2,1)}, bf16[96,1536]{1,0:T(8,128)(2,1)S(1)}, u32[]{:S(2)}, u32[]{:S(2)}) collective-permute-start(bf16[96,1536]{1,0:T(8,128)(2,1)} %get-tuple-element.166), channel_id=1, source_target_pairs={{0,16},{4,20},{8,24},{12,28},{16,0},{20,4},{24,8},{28,12},{1,17},{... | collective-permute-start | bytes 884744 | tf_op jit(solution)/shard_map/ppermute | solution.py:36
  285.5 21.2 %collective-permute-start.55 = (bf16[96,1536]{1,0:T(8,128)(2,1)}, bf16[96,1536]{1,0:T(8,128)(2,1)S(1)}, u32[]{:S(2)}, u32[]{:S(2)}) collective-permute-start(bf16[96,1536]{1,0:T(8,128)(2,1)} %get-tuple-element.167), channel_id=1, source_target_pairs={{0,24},{4,28},{8,16},{12,20},{16,8},{20,12},{24,0},{28,4},{1,25},{... | collective-permute-start | bytes 884744 | tf_op jit(solution)/shard_map/ppermute | solution.py:36
  286.8 26.1 %collective-permute-start.44 = (f32[2,768]{1,0:T(2,128)S(1)}, f32[2,768]{1,0:T(2,128)S(1)}, u32[]{:S(2)}, u32[]{:S(2)}) collective-permute-start(f32[2,768]{1,0:T(2,128)S(1)} %add.122), channel_id=1, source_target_pairs={{0,16},{4,20},{8,24},{12,28},{16,0},{20,4},{24,8},{28,12},{1,17},{... | collective-permute-start | bytes 18440 | tf_op jit(solution)/shard_map/ppermute | solution.py:36
  312.9 21.9 %collective-permute-start.45 = (f32[2,768]{1,0:T(2,128)S(1)}, f32[2,768]{1,0:T(2,128)S(1)}, u32[]{:S(2)}, u32[]{:S(2)}) collective-permute-start(f32[2,768]{1,0:T(2,128)S(1)} %add.123), channel_id=1, source_target_pairs={{0,4},{4,0},{8,12},{12,8},{16,20},{20,16},{24,28},{28,24},{1,5},{5... | collective-permute-start | bytes 18440 | tf_op jit(solution)/shard_map/ppermute | solution.py:36
  335.4 28.3 %collective-permute-start.38 = (bf16[512,768]{1,0:T(8,128)(2,1)S(1)}, bf16[512,768]{1,0:T(8,128)(2,1)S(1)}, u32[]{:S(2)}, u32[]{:S(2)}) collective-permute-start(bf16[512,768]{1,0:T(8,128)(2,1)S(1)} %copy-done.50), channel_id=1, source_target_pairs={{0,1},{1,0},{2,3},{3,2},{4,5},{5,4},{6,7},{7,6},{8,9},{9,8},{10,11... | collective-permute-start | bytes 2359304 | tf_op jit(solution)/shard_map/ppermute | solution.py:36
  338.8 24.9 %collective-permute-start.40 = (bf16[512,768]{1,0:T(8,128)(2,1)S(1)}, bf16[512,768]{1,0:T(8,128)(2,1)S(1)}, u32[]{:S(2)}, u32[]{:S(2)}) collective-permute-start(bf16[512,768]{1,0:T(8,128)(2,1)S(1)} %add_convert_fusion), channel_id=1, source_target_pairs={{0,2},{1,3},{2,0},{3,1},{4,6},{5,7},{6,4},{7,5},{8,10},{9,11},{10,... | collective-permute-start | bytes 2359304 | tf_op jit(solution)/shard_map/ppermute | solution.py:36
  (86 other events, 811.0 us)

commit v2 on v1

--- a/solution.py
+++ b/solution.py
@@ -221,6 +221,7 @@
         a = jnp.concatenate([q, k, v, o.T, gain_one[:, None], gain_two[:, None]], axis=1)
         return jnp.pad(a, ((0, 0), (0, first - a.shape[1]))), jnp.concatenate([gate, up, down], axis=1)
     args = (q, k, v, o, gain_one[None], gain_two[None], gate, up, down)
+    args = tuple(pltpu.with_memory_space_constraint(arg, pltpu.HBM) for arg in args)
     return call(
         pack_kernel,
         (1,),
@@ -282,18 +283,16 @@
         del refs[:count]
         return pick(taken, steps)
 
-    found = []
+    @pl.when(step == 0)
+    def _():
+        total[...] = jnp.zeros_like(total)
+
+    at = 0
     for lhs_parts, rhs_parts in groups:
         lhs = take(lhs_parts)
-        found.append(dot(lhs, jnp.concatenate([take(count) for count in rhs_parts], axis=1), TN))
-
-    @pl.when(step == 0)
-    def _():
-        total[...] = jnp.concatenate(found, axis=1)
-
-    @pl.when(step > 0)
-    def _():
-        total[...] += jnp.concatenate(found, axis=1)
+        rhs = jnp.concatenate([take(count) for count in rhs_parts], axis=1)
+        total[:, at : at + rhs.shape[1]] += dot(lhs, rhs, TN)
+        at += rhs.shape[1]
 
     @pl.when(step == steps - 1)
     def _():
@@ -486,12 +485,6 @@
     m = wide32(pick(xs, steps))
     for o_ref, out_ref in zip(os, ws):
         m = m + dot(o_ref[...], out_ref[:, :heads_width], NT)
-    if near:
-
-        @pl.when(pl.program_id(0) < steps // 2)
-        def _():
-            outs[8][...] = m
-
     n = m * inverse_rms(m)
     h = low(n * gain_ref[1:2, :])
     h_ref[...] = h
@@ -505,14 +498,20 @@
     slope = half + (0.5 * scale) * gate * (1.0 - t * t) * (1.0 + 0.134145 * square)
     hid = low(act * up)
     hid_ref[...] = hid
-    put(ys, low(dot(hid, w_ref[:, 2 * width :], NT)), steps)
+    y = low(dot(hid, w_ref[:, 2 * width :], NT))
     dhid = dot(pick(gs, steps), w_ref[:, 2 * width :])
     dgate = low(dhid * up * slope)
     dup = low(dhid * act)
     dg_ref[...] = dgate
     du_ref[...] = dup
     dh = dot(dgate, w_ref[:, :width], NT) + dot(dup, w_ref[:, width : 2 * width], NT)
+    put(ys, y, steps)
     put(dhs, low(dh), steps)
+    if near:
+
+        @pl.when(pl.program_id(0) < steps // 2)
+        def _():
+            outs[8][...] = m
 
 
 def mlp(place, xs, gs, os, out_ws, gains, weight, near, block=256):
@@ -577,10 +576,11 @@
     )
     attn_pieces = gather_wide(attn_own)
     x = gather_rows(patches, attn_pieces[2:3])
-    mlp_pieces = gather_wide(after(mlp_own, *attn_pieces[1:4]), attn_pieces[4:])
+    mlp_own = after(mlp_own, *attn_pieces[1:4])
     g = gather_rows(after(cotangent, *attn_pieces[1:4]))
 
     h_one, q, k, v, qkv_w, out_w, gains = project(place, x, attn_pieces, width)
+    mlp_pieces = gather_wide(mlp_own, [gains])
     out_ws = gather_rows(after(out_w, g[2]))
     half = q.shape[0] // 2
     o_near, lse_near = attention_forward(scalars, q, k, v, 0)

time: 368 us -> 356 us (0.967)
  starting transfers between devices: 63 us -> 53.4 us
  local copies, waits for them, and re-layouts: 17 us -> 11 us
  waiting for transfers between devices: 120 us -> 126 us
    ppermute x58, starting transfers between devices: 63 us -> 53.4 us  [swap(): return lax.ppermute(values, axis, [(i, i ^ bits) for i in range(size)])]
    ppermute x58, waiting for transfers between devices: 120 us -> 126 us  [swap(): return lax.ppermute(values, axis, [(i, i ^ bits) for i in range(size)])]
    unnamed x104 -> x86, local copies, waits for them, and re-layouts: 16.5 us -> 10.5 us
  transfers between devices with their start and end apart: 58 -> 58, of which waited for: 21 -> 20; matrix products, arithmetic and copies ran while one was open for 3% -> 3% of each run, Pallas kernels for 41% -> 42%
where the time goes in v2:
time: 356 us; the launch traced here: 355 us
  Pallas kernels  149 us (42%)
  waiting for transfers between devices  126 us (35%)
  starting transfers between devices  53.4 us (15%)
  other arithmetic  14.2 us (4%)
  local copies, waits for them, and re-layouts  11 us (3%)
    ppermute x58, waiting for transfers between devices, swap(): return lax.ppermute(values, axis, [(i, i ^ bits) for i in range(size)])  126 us
    ppermute x58, starting transfers between devices, swap(): return lax.ppermute(values, axis, [(i, i ^ bits) for i in range(size)])  53.4 us
    pallas_call x2, Pallas kernels, attention_backward(): call(functools.partial(backward_kernel, first=first, block=block, heads=h...  45.3 us
    pallas_call x2, Pallas kernels, mlp(): call(functools.partial(mlp_kernel, width=width, heads_width=heads_width,...  32.2 us
    pallas_call x2, Pallas kernels, attention_forward(): call(functools.partial(forward_kernel, first=first, block=block, heads=he...  26.8 us
    pallas_call x3, Pallas kernels, grad_pieces(): call(functools.partial(grads_kernel, groups=counts, steps=tokens // block...  23.9 us
    unnamed x86, local copies, waits for them, and re-layouts  10.5 us
    pallas_call x2, Pallas kernels, rows_back(): call(functools.partial(rows_kernel, width=width, steps=steps), (steps,),...  8.79 us
  transfers between devices with their start and end apart: 58, of which 20 were waited for; matrix products, arithmetic and copies ran while one was open for 3% of the time, Pallas kernels for 42%

profile of v2, /device:TPU:0, one launch (start us, length us, event | category | flops | bytes accessed | tf_op | source)
XLA Modules:
  0.0 355.0 jit_solution(11441636555205302347)
XLA Ops:
  9.7 4.7 %collective-permute-done.3.refs_7_ = bf16[96,896]{1,0:T(8,128)(2,1)S(1)} collective-permute-done((bf16[96,896]{1,0:T(8,128)(2,1)S(1)}, bf16[96,896]{1,0:T(8,128)(2,1)S(1)}, u32[]{:S(2)}, u32[]{:S(2)}) %collective-permute-start.3) | collective-permute-done | bytes 172064 | tf_op jit(solution)/shard_map/ppermute | solution.py:36
  17.6 5.6 %collective-permute-done.refs_6_ = bf16[96,896]{1,0:T(8,128)(2,1)S(1)} collective-permute-done((bf16[96,896]{1,0:T(8,128)(2,1)S(1)}, bf16[96,896]{1,0:T(8,128)(2,1)S(1)}, u32[]{:S(2)}, u32[]{:S(2)}) %collective-permute-start) | collective-permute-done | bytes 172064 | tf_op jit(solution)/shard_map/ppermute | solution.py:36
  26.2 5.2 %collective-permute-done.7.refs_8_ = bf16[96,896]{1,0:T(8,128)(2,1)S(1)} collective-permute-done((bf16[96,896]{1,0:T(8,128)(2,1)S(1)}, bf16[96,896]{1,0:T(8,128)(2,1)S(1)}, u32[]{:S(2)}, u32[]{:S(2)}) %collective-permute-start.7) | collective-permute-done | bytes 172064 | tf_op jit(solution)/shard_map/ppermute | solution.py:36
  35.7 6.3 %collective-permute-done.14.refs_2_.refs_10_ = bf16[512,768]{1,0:T(8,128)(2,1)S(1)} collective-permute-done((bf16[512,768]{1,0:T(8,128)(2,1)}, bf16[512,768]{1,0:T(8,128)(2,1)S(1)}, u32[]{:S(2)}, u32[]{:S(2)}) %collective-permute-start.14) | collective-permute-done | bytes 786464 | tf_op jit(solution)/shard_map/ppermute | solution.py:36
  52.2 8.6 %shard_map.222 = (bf16[2048,768]{1,0:T(8,128)(2,1)}, bf16[2048,192]{1,0:T(8,128)(2,1)}, bf16[2048,192]{1,0:T(8,128)(2,1)}, bf16[2048,192]{1,0:T(8,128)(2,1)}, bf...) custom-call(s32[8]{0:T(128)S(1)} %broadcast_xor_fusion.place_ref, ...), custom_call_target="tpu_custom_call" | custom-call | tf_op jit(solution)/shard_map/pallas_call | solution.py:263
  60.8 13.4 %shard_map.223 = (bf16[1024,192]{1,0:T(8,128)(2,1)S(1)}, f32[1024,3]{1,0:T(8,128)S(1)}) custom-call(s32[1,4]{1,0:T(1,128)S(1)} %copy-done.15, s32[1,4]{1,0:T(1,128)S(1)} %copy-done.16, s32[1]{0:T(128)} %bitcast.3.own_ref, bf16[2048,192]{1,0:T(8,128)(2,1)} %get-tuple-element.90.q_ref, bf16[2048,192]{1,0:T(8,128)(2,1)} %get-tuple-element.91.k_ref, ...), custom_call_target="tpu_custom_call" | custom-call | tf_op jit(solution)/shard_map/pallas_call | solution.py:408
  78.4 13.4 %shard_map.224 = (bf16[1024,192]{1,0:T(8,128)(2,1)S(1)}, f32[1024,3]{1,0:T(8,128)S(1)}) custom-call(s32[1,4]{1,0:T(1,128)S(1)} %copy-done.15, s32[1,4]{1,0:T(1,128)S(1)} %copy-done.16, s32[1]{0:T(128)} %bitcast.3.own_ref, bf16[2048,192]{1,0:T(8,128)(2,1)} %get-tuple-element.90.q_ref, bf16[2048,192]{1,0:T(8,128)(2,1)} %get-tuple-element.91.k_ref, ...), custom_call_target="tpu_custom_call" | custom-call | tf_op jit(solution)/shard_map/pallas_call | solution.py:408
  93.5 7.9 %collective-permute-done.25.refs_17_ = bf16[96,1536]{1,0:T(8,128)(2,1)S(1)} collective-permute-done((bf16[96,1536]{1,0:T(8,128)(2,1)S(1)}, bf16[96,1536]{1,0:T(8,128)(2,1)S(1)}, u32[]{:S(2)}, u32[]{:S(2)}) %collective-permute-start.25) | collective-permute-done | bytes 294944 | tf_op jit(solution)/shard_map/ppermute | solution.py:36
  103.7 16.3 %shard_map.225 = (bf16[512,768]{1,0:T(8,128)(2,1)}, bf16[512,768]{1,0:T(8,128)(2,1)}, bf16[512,768]{1,0:T(8,128)(2,1)}, bf16[512,768]{1,0:T(8,128)(2,1)}, bf16[1...) custom-call(s32[8]{0:T(128)S(1)} %broadcast_xor_fusion.place_ref, ...), custom_call_target="tpu_custom_call" | custom-call | tf_op jit(solution)/shard_map/pallas_call | solution.py:524
  128.9 16.0 %shard_map.226 = (bf16[512,768]{1,0:T(8,128)(2,1)}, bf16[512,768]{1,0:T(8,128)(2,1)}, bf16[512,768]{1,0:T(8,128)(2,1)}, bf16[512,768]{1,0:T(8,128)(2,1)}, bf16[1...) custom-call(s32[8]{0:T(128)S(1)} %broadcast_xor_fusion.place_ref, ...), custom_call_target="tpu_custom_call" | custom-call | tf_op jit(solution)/shard_map/pallas_call | solution.py:524
  147.4 17.7 %collective-permute-done.33 = bf16[512,768]{1,0:T(8,128)(2,1)S(1)} collective-permute-done((bf16[512,768]{1,0:T(8,128)(2,1)S(1)}, bf16[512,768]{1,0:T(8,128)(2,1)S(1)}, u32[]{:S(2)}, u32[]{:S(2)}) %collective-permute-start.33) | collective-permute-done | bytes 786464 | tf_op jit(solution)/shard_map/ppermute | solution.py:36
  169.7 17.4 %collective-permute-done.34.ga_ref.refs_2_ = bf16[512,768]{1,0:T(8,128)(2,1)S(1)} collective-permute-done((bf16[512,768]{1,0:T(8,128)(2,1)S(1)}, bf16[512,768]{1,0:T(8,128)(2,1)S(1)}, u32[]{:S(2)}, u32[]{:S(2)}) %collective-permute-start.34) | collective-permute-done | bytes 786464 | tf_op jit(solution)/shard_map/ppermute | solution.py:36
  187.6 12.4 %shard_map.232 = (bf16[96,1536]{1,0:T(8,128)(2,1)S(1)}, bf16[96,1536]{1,0:T(8,128)(2,1)S(1)}, bf16[96,1536]{1,0:T(8,128)(2,1)S(1)}, bf16[96,1536]{1,0:T(8,128)(2...) custom-call(s32[8]{0:T(128)S(1)} %broadcast_xor_fusion.place_ref, ...), custom_call_target="tpu_custom_call" | custom-call | tf_op jit(solution)/shard_map/pallas_call | solution.py:330
  203.4 21.8 %shard_map.227 = (bf16[1024,192]{1,0:T(8,128)(2,1)S(1)}, f32[192,2048]{1,0:T(8,128)}, f32[192,2048]{1,0:T(8,128)}) custom-call(s32[1,4]{1,0:T(1,128)S(1)} %copy-done.15, s32[1,4]{1,0:T(1,128)S(1)} %copy-done.16, s32[1]{0:T(128)} %bitcast.3.own_ref, bf16[2048,192]{1,0:T(8,128)(2,1)} %get-tuple-element.90.q_ref, bf16[2048,192]{1,0:T(8,128)(2,1)} %get-tuple-element.91.k_ref, ...), custom_call_target="tpu_custom_call" | custom-call | tf_op jit(solution)/shard_map/pallas_call | solution.py:463
  226.1 23.5 %shard_map.228 = (bf16[1024,192]{1,0:T(8,128)(2,1)S(1)}, bf16[2048,192]{1,0:T(8,128)(2,1)}, bf16[2048,192]{1,0:T(8,128)(2,1)}) custom-call(s32[1,4]{1,0:T(1,128)S(1)} %copy-done.15, s32[1,4]{1,0:T(1,128)S(1)} %copy-done.16, s32[1]{0:T(128)} %bitcast.3.own_ref, bf16[2048,192]{1,0:T(8,128)(2,1)} %get-tuple-element.90.q_ref, ...), custom_call_target="tpu_custom_call" | custom-call | tf_op jit(solution)/shard_map/pallas_call | solution.py:463
  250.4 7.0 %shard_map.231 = (bf16[96,576]{1,0:T(8,128)(2,1)S(1)}, bf16[96,576]{1,0:T(8,128)(2,1)S(1)}, bf16[96,576]{1,0:T(8,128)(2,1)S(1)}, bf16[96,576]{1,0:T(8,128)(2,1)S...) custom-call(s32[8]{0:T(128)S(1)} %broadcast_xor_fusion.place_ref, ...), custom_call_target="tpu_custom_call" | custom-call | tf_op jit(solution)/shard_map/pallas_call | solution.py:330
  266.0 6.2 %collective-permute-done.43 = f32[2,768]{1,0:T(2,128)S(1)} collective-permute-done((f32[2,768]{1,0:T(2,128)S(1)}, f32[2,768]{1,0:T(2,128)S(1)}, u32[]{:S(2)}, u32[]{:S(2)}) %collective-permute-start.43) | collective-permute-done | bytes 6176 | tf_op jit(solution)/shard_map/ppermute | solution.py:36
  277.2 17.6 %collective-permute-done.56.refs_2_ = bf16[96,1536]{1,0:T(8,128)(2,1)S(1)} collective-permute-done((bf16[96,1536]{1,0:T(8,128)(2,1)}, bf16[96,1536]{1,0:T(8,128)(2,1)S(1)}, u32[]{:S(2)}, u32[]{:S(2)}) %collective-permute-start.56) | collective-permute-done | bytes 294944 | tf_op jit(solution)/shard_map/ppermute | solution.py:36
  295.6 5.5 %collective-permute-done.44 = f32[2,768]{1,0:T(2,128)S(1)} collective-permute-done((f32[2,768]{1,0:T(2,128)S(1)}, f32[2,768]{1,0:T(2,128)S(1)}, u32[]{:S(2)}, u32[]{:S(2)}) %collective-permute-start.44) | collective-permute-done | bytes 6176 | tf_op jit(solution)/shard_map/ppermute | solution.py:36
  304.6 4.3 %shard_map.230 = (bf16[512,768]{1,0:T(8,128)(2,1)S(1)}, bf16[512,768]{1,0:T(8,128)(2,1)}) custom-call(bf16[1024,192]{1,0:T(8,128)(2,1)S(1)} %copy-done.8, bf16[2048,192]{1,0:T(8,128)(2,1)} %get-tuple-element.117.dk_ref.refs_5_, bf16[2048,192]{1,0:T(8,128)(2,1)} %get-tuple-element.118.dv_ref.refs_6_, bf16[768,896]{1,0:T(8,128)(2,1)} %get-tuple-element.119.w_ref.refs_0_), custom_call_target="tpu_custom_call" | custom-call | tf_op jit(solution)/shard_map/pallas_call | solution.py:549
  308.9 4.4 %shard_map.229 = (bf16[512,768]{1,0:T(8,128)(2,1)S(1)}, bf16[512,768]{1,0:T(8,128)(2,1)}) custom-call(bf16[1024,192]{1,0:T(8,128)(2,1)S(1)} %get-tuple-element.113.dq_ref.refs_3_, bf16[2048,192]{1,0:T(8,128)(2,1)} %get-tuple-element.117.dk_ref.refs_5_, bf16[2048,192]{1,0:T(8,128)(2,1)} %get-tuple-element.118.dv_ref.refs_6_, ...), custom_call_target="tpu_custom_call" | custom-call | tf_op jit(solution)/shard_map/pallas_call | solution.py:549
  313.4 4.4 %shard_map.233 = (bf16[96,192]{1,0:T(8,128)(2,1)S(1)}, bf16[96,192]{1,0:T(8,128)(2,1)S(1)}, bf16[96,192]{1,0:T(8,128)(2,1)S(1)}, bf16[96,192]{1,0:T(8,128)(2,1)S...) custom-call(s32[8]{0:T(128)S(1)} %broadcast_xor_fusion.place_ref, bf16[512,768]{1,0:T(8,128)(2,1)} %copy-done.23, ...), custom_call_target="tpu_custom_call" | custom-call | tf_op jit(solution)/shard_map/pallas_call | solution.py:330
  327.8 7.5 %collective-permute-done.48 = bf16[288,576]{1,0:T(8,128)(2,1)S(1)} collective-permute-done((bf16[288,576]{1,0:T(8,128)(2,1)S(1)}, bf16[288,576]{1,0:T(8,128)(2,1)S(1)}, u32[]{:S(2)}, u32[]{:S(2)}) %collective-permute-start.48) | collective-permute-done | bytes 331808 | tf_op jit(solution)/shard_map/ppermute | solution.py:36
  344.1 6.9 %collective-permute-done.51.refs_2_ = bf16[96,768]{1,0:T(8,128)(2,1)S(1)} collective-permute-done((bf16[96,768]{1,0:T(8,128)(2,1)S(1)}, bf16[96,768]{1,0:T(8,128)(2,1)S(1)}, u32[]{:S(2)}, u32[]{:S(2)}) %collective-permute-start.51) | collective-permute-done | bytes 147488 | tf_op jit(solution)/shard_map/ppermute | solution.py:36
  (228 shorter events, 99.7 us)
Async XLA Ops:
  0.6 23.0 %collective-permute-start.5 = (bf16[512,768]{1,0:T(8,128)(2,1)}, bf16[512,768]{1,0:T(8,128)(2,1)}, u32[]{:S(2)}, u32[]{:S(2)}) collective-permute-start(bf16[512,768]{1,0:T(8,128)(2,1)} %refs_0_.5), channel_id=1, source_target_pairs={{0,2},{1,3},{2,0},{3,1},{4,6},{5,7},{6,4},{7,5},{8,10},{9,11},{10,... | collective-permute-start | bytes 2359304 | tf_op jit(solution)/shard_map/ppermute | solution.py:36
  23.7 26.3 %collective-permute-start.1 = (bf16[512,768]{1,0:T(8,128)(2,1)}, bf16[512,768]{1,0:T(8,128)(2,1)}, u32[]{:S(2)}, u32[]{:S(2)}) collective-permute-start(bf16[512,768]{1,0:T(8,128)(2,1)} %refs_0_.5), channel_id=1, source_target_pairs={{0,1},{1,0},{2,3},{3,2},{4,5},{5,4},{6,7},{7,6},{8,9},{9,8},{10,11... | collective-permute-start | bytes 2359304 | tf_op jit(solution)/shard_map/ppermute | solution.py:36
  23.7 28.5 %collective-permute-start.6 = (bf16[512,768]{1,0:T(8,128)(2,1)}, bf16[512,768]{1,0:T(8,128)(2,1)}, u32[]{:S(2)}, u32[]{:S(2)}) collective-permute-start(bf16[512,768]{1,0:T(8,128)(2,1)} %collective-permute-done.5.refs_2_.refs_0_), channel_id=1, source_target_pairs={{0,1},{1,0},{2,3},{3,2},{4,5},{5,4},{6,7},{7,6},{8,9},{9,8},{10,11... | collective-permute-start | bytes 2359304 | tf_op jit(solution)/shard_map/ppermute | solution.py:36
  43.5 49.4 %collective-permute-start.18 = (bf16[512,768]{1,0:T(8,128)(2,1)S(1)}, bf16[512,768]{1,0:T(8,128)(2,1)}, u32[]{:S(2)}, u32[]{:S(2)}) collective-permute-start(bf16[512,768]{1,0:T(8,128)(2,1)S(1)} %collective-permute-done.14.refs_2_.refs_10_), channel_id=1, source_target_pairs={{0,1},{1,0},{2,3},{3,2},{4,5},{5,4},{6,7},{7,6},{8,9},{9,8},{10,11... | collective-permute-start | bytes 2359304 | tf_op jit(solution)/shard_map/ppermute | solution.py:36
  47.4 27.4 %collective-permute-start.23 = (bf16[96,1536]{1,0:T(8,128)(2,1)S(1)}, bf16[96,1536]{1,0:T(8,128)(2,1)S(1)}, u32[]{:S(2)}, u32[]{:S(2)}) collective-permute-start(bf16[96,1536]{1,0:T(8,128)(2,1)S(1)} %get-tuple-element.100.refs_13_), channel_id=1, source_target_pairs={{0,16},{4,20},{8,24},{12,28},{16,0},{20,4},{24,8},{28,12},{1,17},{... | collective-permute-start | bytes 884744 | tf_op jit(solution)/shard_map/ppermute | solution.py:36
  47.4 27.9 %collective-permute-start.22 = (bf16[96,1536]{1,0:T(8,128)(2,1)S(1)}, bf16[96,1536]{1,0:T(8,128)(2,1)S(1)}, u32[]{:S(2)}, u32[]{:S(2)}) collective-permute-start(bf16[96,1536]{1,0:T(8,128)(2,1)S(1)} %get-tuple-element.100.refs_13_), channel_id=1, source_target_pairs={{0,8},{4,12},{8,0},{12,4},{16,24},{20,28},{24,16},{28,20},{1,9},{5... | collective-permute-start | bytes 884744 | tf_op jit(solution)/shard_map/ppermute | solution.py:36
  50.0 26.8 %collective-permute-start.28 = (bf16[96,1536]{1,0:T(8,128)(2,1)S(1)}, bf16[96,1536]{1,0:T(8,128)(2,1)}, u32[]{:S(2)}, u32[]{:S(2)}) collective-permute-start(bf16[96,1536]{1,0:T(8,128)(2,1)S(1)} %collective-permute-done.24.refs_16_), channel_id=1, source_target_pairs={{0,4},{4,0},{8,12},{12,8},{16,20},{20,16},{24,28},{28,24},{1,5},{5... | collective-permute-start | bytes 884744 | tf_op jit(solution)/shard_map/ppermute | solution.py:36
  101.4 19.3 %collective-permute-start.4 = (bf16[512,768]{1,0:T(8,128)(2,1)S(1)}, bf16[512,768]{1,0:T(8,128)(2,1)S(1)}, u32[]{:S(2)}, u32[]{:S(2)}) collective-permute-start(bf16[512,768]{1,0:T(8,128)(2,1)S(1)} %copy-done.21), channel_id=1, source_target_pairs={{0,1},{1,0},{2,3},{3,2},{4,5},{5,4},{6,7},{7,6},{8,9},{9,8},{10,11... | collective-permute-start | bytes 2359304 | tf_op jit(solution)/shard_map/ppermute | solution.py:36
  101.4 19.2 %collective-permute-start.12 = (bf16[1024,192]{1,0:T(8,128)(2,1)S(1)}, bf16[1024,192]{1,0:T(8,128)(2,1)S(1)}, u32[]{:S(2)}, u32[]{:S(2)}) collective-permute-start(bf16[1024,192]{1,0:T(8,128)(2,1)S(1)} %get-tuple-element.94.refs_4_.o_ref.refs_5_), channel_id=1, source_target_pairs={{0,2},{1,3},{2,0},{3,1},{4,6},{5,7},{6,4},{7,5},{8,10},{9,11},{10,... | collective-permute-start | bytes 1179656 | tf_op jit(solution)/shard_map/ppermute | solution.py:36
  120.0 25.1 %collective-permute-start.32 = (bf16[512,768]{1,0:T(8,128)(2,1)}, bf16[512,768]{1,0:T(8,128)(2,1)S(1)}, u32[]{:S(2)}, u32[]{:S(2)}) collective-permute-start(bf16[512,768]{1,0:T(8,128)(2,1)} %get-tuple-element.110), channel_id=1, source_target_pairs={{0,1},{1,0},{2,3},{3,2},{4,5},{5,4},{6,7},{7,6},{8,9},{9,8},{10,11... | collective-permute-start | bytes 2359304 | tf_op jit(solution)/shard_map/ppermute | solution.py:36
  145.3 19.9 %collective-permute-start.33 = (bf16[512,768]{1,0:T(8,128)(2,1)S(1)}, bf16[512,768]{1,0:T(8,128)(2,1)S(1)}, u32[]{:S(2)}, u32[]{:S(2)}) collective-permute-start(bf16[512,768]{1,0:T(8,128)(2,1)S(1)} %add_convert_fusion.2), channel_id=1, source_target_pairs={{0,2},{1,3},{2,0},{3,1},{4,6},{5,7},{6,4},{7,5},{8,10},{9,11},{10,... | collective-permute-start | bytes 2359304 | tf_op jit(solution)/shard_map/ppermute | solution.py:36
  169.7 32.8 %collective-permute-start.36 = (bf16[512,768]{1,0:T(8,128)(2,1)S(1)}, bf16[512,768]{1,0:T(8,128)(2,1)S(1)}, u32[]{:S(2)}, u32[]{:S(2)}) collective-permute-start(bf16[512,768]{1,0:T(8,128)(2,1)S(1)} %get-tuple-element.163.ga_ref.refs_0_), channel_id=1, source_target_pairs={{0,1},{1,0},{2,3},{3,2},{4,5},{5,4},{6,7},{7,6},{8,9},{9,8},{10,11... | collective-permute-start | bytes 2359304 | tf_op jit(solution)/shard_map/ppermute | solution.py:36
  187.1 38.1 %collective-permute-start.37 = (bf16[512,768]{1,0:T(8,128)(2,1)S(1)}, bf16[512,768]{1,0:T(8,128)(2,1)S(1)}, u32[]{:S(2)}, u32[]{:S(2)}) collective-permute-start(bf16[512,768]{1,0:T(8,128)(2,1)S(1)} %collective-permute-done.34.ga_ref.refs_2_), channel_id=1, source_target_pairs={{0,1},{1,0},{2,3},{3,2},{4,5},{5,4},{6,7},{7,6},{8,9},{9,8},{10,11... | collective-permute-start | bytes 2359304 | tf_op jit(solution)/shard_map/ppermute | solution.py:36
  187.1 72.0 %collective-permute-start.30 = (bf16[512,768]{1,0:T(8,128)(2,1)S(1)}, bf16[512,768]{1,0:T(8,128)(2,1)}, u32[]{:S(2)}, u32[]{:S(2)}) collective-permute-start(bf16[512,768]{1,0:T(8,128)(2,1)S(1)} %copy-done.40), channel_id=1, source_target_pairs={{0,1},{1,0},{2,3},{3,2},{4,5},{5,4},{6,7},{7,6},{8,9},{9,8},{10,11... | collective-permute-start | bytes 2359304 | tf_op jit(solution)/shard_map/ppermute | solution.py:36
  200.1 61.3 %collective-permute-start.54 = (bf16[288,1536]{1,0:T(8,128)(2,1)}, bf16[288,1536]{1,0:T(8,128)(2,1)S(1)}, u32[]{:S(2)}, u32[]{:S(2)}) collective-permute-start(bf16[288,1536]{1,0:T(8,128)(2,1)} %get-tuple-element.155), channel_id=1, source_target_pairs={{0,4},{4,0},{8,12},{12,8},{16,20},{20,16},{24,28},{28,24},{1,5},{5... | collective-permute-start | bytes 2654216 | tf_op jit(solution)/shard_map/ppermute | solution.py:36
  200.9 71.9 %collective-permute-start.53 = (bf16[96,1536]{1,0:T(8,128)(2,1)S(1)}, bf16[96,1536]{1,0:T(8,128)(2,1)}, u32[]{:S(2)}, u32[]{:S(2)}) collective-permute-start(bf16[96,1536]{1,0:T(8,128)(2,1)S(1)} %get-tuple-element.153), channel_id=1, source_target_pairs={{0,4},{4,0},{8,12},{12,8},{16,20},{20,16},{24,28},{28,24},{1,5},{5... | collective-permute-start | bytes 884744 | tf_op jit(solution)/shard_map/ppermute | solution.py:36
  202.5 99.1 %collective-permute-start.29 = (bf16[512,768]{1,0:T(8,128)(2,1)}, bf16[512,768]{1,0:T(8,128)(2,1)}, u32[]{:S(2)}, u32[]{:S(2)}) collective-permute-start(bf16[512,768]{1,0:T(8,128)(2,1)} %get-tuple-element.104), channel_id=1, source_target_pairs={{0,1},{1,0},{2,3},{3,2},{4,5},{5,4},{6,7},{7,6},{8,9},{9,8},{10,11... | collective-permute-start | bytes 2359304 | tf_op jit(solution)/shard_map/ppermute | solution.py:36
  262.5 39.1 %collective-permute-start.35 = (bf16[512,768]{1,0:T(8,128)(2,1)}, bf16[512,768]{1,0:T(8,128)(2,1)}, u32[]{:S(2)}, u32[]{:S(2)}) collective-permute-start(bf16[512,768]{1,0:T(8,128)(2,1)} %convert_add_fusion), channel_id=1, source_target_pairs={{0,2},{1,3},{2,0},{3,1},{4,6},{5,7},{6,4},{7,5},{8,10},{9,11},{10,... | collective-permute-start | bytes 2359304 | tf_op jit(solution)/shard_map/ppermute | solution.py:36
  272.2 22.6 %collective-permute-start.56 = (bf16[96,1536]{1,0:T(8,128)(2,1)}, bf16[96,1536]{1,0:T(8,128)(2,1)S(1)}, u32[]{:S(2)}, u32[]{:S(2)}) collective-permute-start(bf16[96,1536]{1,0:T(8,128)(2,1)} %get-tuple-element.166), channel_id=1, source_target_pairs={{0,16},{4,20},{8,24},{12,28},{16,0},{20,4},{24,8},{28,12},{1,17},{... | collective-permute-start | bytes 884744 | tf_op jit(solution)/shard_map/ppermute | solution.py:36
  272.8 21.9 %collective-permute-start.55 = (bf16[96,1536]{1,0:T(8,128)(2,1)}, bf16[96,1536]{1,0:T(8,128)(2,1)S(1)}, u32[]{:S(2)}, u32[]{:S(2)}) collective-permute-start(bf16[96,1536]{1,0:T(8,128)(2,1)} %get-tuple-element.167), channel_id=1, source_target_pairs={{0,24},{4,28},{8,16},{12,20},{16,8},{20,12},{24,0},{28,4},{1,25},{... | collective-permute-start | bytes 884744 | tf_op jit(solution)/shard_map/ppermute | solution.py:36
  274.9 26.2 %collective-permute-start.44 = (f32[2,768]{1,0:T(2,128)S(1)}, f32[2,768]{1,0:T(2,128)S(1)}, u32[]{:S(2)}, u32[]{:S(2)}) collective-permute-start(f32[2,768]{1,0:T(2,128)S(1)} %add.122), channel_id=1, source_target_pairs={{0,16},{4,20},{8,24},{12,28},{16,0},{20,4},{24,8},{28,12},{1,17},{... | collective-permute-start | bytes 18440 | tf_op jit(solution)/shard_map/ppermute | solution.py:36
  301.1 20.8 %collective-permute-start.45 = (f32[2,768]{1,0:T(2,128)S(1)}, f32[2,768]{1,0:T(2,128)S(1)}, u32[]{:S(2)}, u32[]{:S(2)}) collective-permute-start(f32[2,768]{1,0:T(2,128)S(1)} %add.123), channel_id=1, source_target_pairs={{0,4},{4,0},{8,12},{12,8},{16,20},{20,16},{24,28},{28,24},{1,5},{5... | collective-permute-start | bytes 18440 | tf_op jit(solution)/shard_map/ppermute | solution.py:36
  322.5 29.3 %collective-permute-start.38 = (bf16[512,768]{1,0:T(8,128)(2,1)S(1)}, bf16[512,768]{1,0:T(8,128)(2,1)S(1)}, u32[]{:S(2)}, u32[]{:S(2)}) collective-permute-start(bf16[512,768]{1,0:T(8,128)(2,1)S(1)} %copy-done.41), channel_id=1, source_target_pairs={{0,1},{1,0},{2,3},{3,2},{4,5},{5,4},{6,7},{7,6},{8,9},{9,8},{10,11... | collective-permute-start | bytes 2359304 | tf_op jit(solution)/shard_map/ppermute | solution.py:36
  326.3 25.5 %collective-permute-start.40 = (bf16[512,768]{1,0:T(8,128)(2,1)S(1)}, bf16[512,768]{1,0:T(8,128)(2,1)S(1)}, u32[]{:S(2)}, u32[]{:S(2)}) collective-permute-start(bf16[512,768]{1,0:T(8,128)(2,1)S(1)} %add_convert_fusion), channel_id=1, source_target_pairs={{0,2},{1,3},{2,0},{3,1},{4,6},{5,7},{6,4},{7,5},{8,10},{9,11},{10,... | collective-permute-start | bytes 2359304 | tf_op jit(solution)/shard_map/ppermute | solution.py:36
  (77 other events, 811.4 us)

commit v3 on v2

--- a/solution.py
+++ b/solution.py
@@ -12,6 +12,8 @@
 EPSILON = 1e-06
 MASKED = -1e30
 NARROW = 4
+WIDE = "wide"
+ACROSS = "narrow"
 
 
 NT = (((1,), (1,)), ((), ()))
@@ -41,53 +43,54 @@
 
 
 def gather_rows(own, ready=()):
-    across = swap(own, "narrow", 2)
+    across = swap(own, ACROSS, 2)
     near, far = after(own, *ready), after(across, *ready)
-    return own, swap(near, "narrow", 1), across, swap(far, "narrow", 1)
+    return own, swap(near, ACROSS, 1), across, swap(far, ACROSS, 1)
 
 
 def pair_sum(parts):
-    return wide32(parts[0]) + wide32(swap(parts[1], "narrow", 1))
+    return wide32(parts[0]) + wide32(swap(parts[1], ACROSS, 1))
 
 
 def cross(values):
-    return wide32(swap(low(values), "narrow", 2))
+    return wide32(swap(low(values), ACROSS, 2))
 
 
 def places():
-    if lax.axis_size("wide") != 8:
+    if lax.axis_size(WIDE) != 8:
         return jnp.arange(8, dtype=jnp.int32)
-    index = lax.axis_index("wide").astype(jnp.int32)
+    index = lax.axis_index(WIDE).astype(jnp.int32)
     order = jnp.array([0, 2, 4, 6, 1, 3, 5, 7], jnp.int32)
     return jnp.bitwise_xor(order, index)
 
 
 def gather_wide(own, ready=()):
-    if lax.axis_size("wide") != 8:
-        return jnp.split(lax.all_gather(own, "wide", axis=0, tiled=True), 8, axis=0)
-    column = [own] + [swap(own, "wide", 2 * k) for k in (1, 2, 3)]
+    if lax.axis_size(WIDE) != 8:
+        return jnp.split(lax.all_gather(own, WIDE, axis=0, tiled=True), 8, axis=0)
+    column = [own] + [swap(own, WIDE, 2 * k) for k in (1, 2, 3)]
     sent = [after(own, *ready)] + column[1:]
-    return column + [swap(piece, "wide", 1) for piece in sent]
+    return column + [swap(piece, WIDE, 1) for piece in sent]
 
 
 def send_x(sent):
-    if lax.axis_size("wide") != 8:
+    if lax.axis_size(WIDE) != 8:
         return sent
-    return [swap(part, "wide", 1) for part in sent]
+    return [swap(part, WIDE, 1) for part in sent]
 
 
 def add_x(kept, received):
     rows = kept[0].shape[0]
     far = [received[0][j * rows : (j + 1) * rows] for j in range(3)]
-    return [low(wide32(mine) + wide32(other)) for mine, other in zip(kept, [received[1]] + far[::-1])]
+    added = [low(wide32(mine) + wide32(other)) for mine, other in zip(kept[1:], far[::-1])]
+    return [low(wide32(kept[0]) + wide32(received[1]))] + added
 
 
 def send_z(column):
-    return [column[0]] + [swap(column[k], "wide", 2 * k) for k in (3, 2, 1)]
+    return [column[0]] + [swap(column[k], WIDE, 2 * k) for k in (3, 2, 1)]
 
 
 def reduce_wide(parts):
-    size = lax.axis_size("wide")
+    size = lax.axis_size(WIDE)
     if size == 8:
         columns = [add_x(kept, received) for kept, received in parts]
         return send_z([jnp.concatenate(pieces, axis=1) for pieces in zip(*columns)])
@@ -97,20 +100,20 @@
         far = [sent[0][j * rows : (j + 1) * rows] for j in range(3)]
         full.append(jnp.concatenate(kept + [sent[1]] + far[::-1], axis=0))
     full = jnp.concatenate(full, axis=1)
-    return list(lax.all_to_all(full.reshape(size, -1, full.shape[1]), "wide", 0, 0, tiled=True))
+    return list(lax.all_to_all(full.reshape(size, -1, full.shape[1]), WIDE, 0, 0, tiled=True))
 
 
 def sum_all(values):
-    values = values + swap(values, "narrow", 2)
-    values = values + swap(values, "narrow", 1)
-    size = lax.axis_size("wide")
+    size = lax.axis_size(WIDE)
     if size != 8:
-        values = lax.psum(values, "wide")
+        values = lax.psum(values, WIDE)
     else:
         for bits in (2, 4, 1):
-            values = values + swap(values, "wide", bits)
+            values = values + swap(values, WIDE, bits)
+    values = values + swap(values, ACROSS, 2)
+    values = values + swap(values, ACROSS, 1)
     rows = values.shape[1] // size
-    return lax.dynamic_slice_in_dim(values, lax.axis_index("wide") * rows, rows, 1)
+    return lax.dynamic_slice_in_dim(values, lax.axis_index(WIDE) * rows, rows, 1)
 
 
 def call(kernel, grid, in_specs, out_specs, out_shape, scratch=(), prefetch=0):
@@ -217,7 +220,7 @@
 def pack(q, k, v, o, gain_one, gain_two, gate, up, down):
     rows, width = q.shape
     first, second = round_up(4 * width + 2), 3 * gate.shape[1]
-    if lax.axis_size("wide") != 8:
+    if lax.axis_size(WIDE) != 8:
         a = jnp.concatenate([q, k, v, o.T, gain_one[:, None], gain_two[:, None]], axis=1)
         return jnp.pad(a, ((0, 0), (0, first - a.shape[1]))), jnp.concatenate([gate, up, down], axis=1)
     args = (q, k, v, o, gain_one[None], gain_two[None], gate, up, down)
@@ -568,7 +571,7 @@
 ):
     width = query_weight.shape[1]
     hidden = gate_weight.shape[1]
-    scalars = (item_len, valid_count, lax.axis_index("narrow").astype(jnp.int32).reshape(1))
+    scalars = (item_len, valid_count, lax.axis_index(ACROSS).astype(jnp.int32).reshape(1))
     place = places()
     attn_own, mlp_own = pack(
         query_weight, key_weight, value_weight, out_weight, norm1_gain, norm2_gain,
@@ -584,12 +587,12 @@
     out_ws = gather_rows(after(out_w, g[2]))
     half = q.shape[0] // 2
     o_near, lse_near = attention_forward(scalars, q, k, v, 0)
-    o_far_across = swap(o_near, "narrow", 2)
-    o_far_across = (o_far_across, swap(o_far_across, "narrow", 1))
+    o_far_across = swap(o_near, ACROSS, 2)
+    o_far_across = (o_far_across, swap(o_far_across, ACROSS, 1))
     o_far, lse_far = attention_forward(scalars, q, k, v, half)
-    o_near_across = swap(o_far, "narrow", 2)
-    o_far_all = (o_far, swap(o_far, "narrow", 1)) + o_far_across
-    o_near_all = (o_near, swap(o_near, "narrow", 1), o_near_across, swap(o_near_across, "narrow", 1))
+    o_near_across = swap(o_far, ACROSS, 2)
+    o_far_all = (o_far, swap(o_far, ACROSS, 1)) + o_far_across
+    o_near_all = (o_near, swap(o_near, ACROSS, 1), o_near_across, swap(o_near_across, ACROSS, 1))
     y_far, dh_far, h2_far, hid_far, dg_far, du_far, mlp_w = mlp(
         place, x[2:], g[2:], o_far_all, out_ws, gains, mlp_pieces, False
     )
@@ -610,7 +613,7 @@
     mlp_pieces = reduce_wide([(mlp_kept, mlp_sent)])
     grad_gate, grad_up, grad_down = finish(mlp_pieces, (hidden, hidden, hidden), False)
     dq_near, dk_sum, dv_sum = attention_backward(scalars, q, k, v, d[:2], out_w, o_near, lse_near, ())
-    output = low(middle_own + pair_sum(y_near) + cross(after(pair_sum(y_far), d[2])))
+    y_from_far = cross(after(pair_sum(y_far), d[2]))
     out_kept, out_sent = grad_pieces(place, [(list(d), [[o_near, o_far]])])
     out_sent = send_x(out_sent)
     dq_far, dk, dv = attention_backward(scalars, q, k, v, d[2:], out_w, o_far, lse_far, (dk_sum, dv_sum))
@@ -626,6 +629,8 @@
         reduce_wide([(attn_kept, attn_sent), (out_kept, out_sent)]), (width, width, width, width), True
     )
     dh_one = pair_sum(dh_near) + from_far
+    y_own = pair_sum((y_near[0], after(y_near[1], dh_near[0])))
+    output = low(middle_own + y_own + y_from_far)
     grad_input = middle_grad_own + norm_back(wide32(patches), gain_one, dh_one)
     return (
         output, grad_input, norms[0], grad_query, grad_key, grad_value, grad_out, norms[1],
@@ -634,19 +639,19 @@
 
 
 def solution(mesh):
-    tokens = P(("wide", "narrow"), None)
+    tokens = P((WIDE, ACROSS), None)
 
     return jax.shard_map(
         on_device,
         mesh=mesh,
         in_specs=(
-            tokens, tokens, P("wide", None), P("wide", None), P("wide"), P("wide", "narrow"),
-            P("wide", "narrow"), P("wide", "narrow"), P("narrow", "wide"), P("wide"),
-            P("wide", "narrow"), P("wide", "narrow"), P("narrow", "wide"),
+            tokens, tokens, P(WIDE, None), P(WIDE, None), P(WIDE), P(WIDE, ACROSS),
+            P(WIDE, ACROSS), P(WIDE, ACROSS), P(ACROSS, WIDE), P(WIDE),
+            P(WIDE, ACROSS), P(WIDE, ACROSS), P(ACROSS, WIDE),
         ),
         out_specs=(
-            tokens, tokens, P("wide"), P("wide", "narrow"), P("wide", "narrow"), P("wide", "narrow"),
-            P("narrow", "wide"), P("wide"), P("wide", "narrow"), P("wide", "narrow"), P("narrow", "wide"),
+            tokens, tokens, P(WIDE), P(WIDE, ACROSS), P(WIDE, ACROSS), P(WIDE, ACROSS),
+            P(ACROSS, WIDE), P(WIDE), P(WIDE, ACROSS), P(WIDE, ACROSS), P(ACROSS, WIDE),
         ),
         check_vma=False,
     )

time: 356 us -> 357 us (level)
    unnamed x86 -> x100, local copies, waits for them, and re-layouts: 10.5 us -> 13.4 us
  transfers between devices with their start and end apart: 58 -> 58, of which waited for: 20 -> 23; matrix products, arithmetic and copies ran while one was open for 3% -> 2% of each run, Pallas kernels for 42% -> 42%
where the time goes in v3:
time: 357 us; the launch traced here: 356 us
  Pallas kernels  149 us (42%)
  waiting for transfers between devices  125 us (35%)
  starting transfers between devices  55.5 us (16%)
  local copies, waits for them, and re-layouts  13.9 us (4%)
  other arithmetic  11.9 us (3%)
    ppermute x58, waiting for transfers between devices, swap(): return lax.ppermute(values, axis, [(i, i ^ bits) for i in range(size)])  125 us
    ppermute x58, starting transfers between devices, swap(): return lax.ppermute(values, axis, [(i, i ^ bits) for i in range(size)])  55.5 us
    pallas_call x2, Pallas kernels, attention_backward(): call(functools.partial(backward_kernel, first=first, block=block, heads=h...  45.4 us
    pallas_call x2, Pallas kernels, mlp(): call(functools.partial(mlp_kernel, width=width, heads_width=heads_width,...  32.2 us
    pallas_call x2, Pallas kernels, attention_forward(): call(functools.partial(forward_kernel, first=first, block=block, heads=he...  26.8 us
    pallas_call x3, Pallas kernels, grad_pieces(): call(functools.partial(grads_kernel, groups=counts, steps=tokens // block...  24.2 us
    unnamed x100, local copies, waits for them, and re-layouts  13.4 us
    pallas_call x2, Pallas kernels, rows_back(): call(functools.partial(rows_kernel, width=width, steps=steps), (steps,),...  8.68 us
  transfers between devices with their start and end apart: 58, of which 23 were waited for; matrix products, arithmetic and copies ran while one was open for 2% of the time, Pallas kernels for 42%

profile of v3, /device:TPU:0, one launch (start us, length us, event | category | flops | bytes accessed | tf_op | source)
XLA Modules:
  0.0 356.4 jit_solution(7349434396531934543)
XLA Ops:
  9.7 4.7 %collective-permute-done.3.refs_7_ = bf16[96,896]{1,0:T(8,128)(2,1)S(1)} collective-permute-done((bf16[96,896]{1,0:T(8,128)(2,1)S(1)}, bf16[96,896]{1,0:T(8,128)(2,1)S(1)}, u32[]{:S(2)}, u32[]{:S(2)}) %collective-permute-start.3) | collective-permute-done | bytes 172064 | tf_op jit(solution)/shard_map/ppermute | solution.py:38
  17.6 5.6 %collective-permute-done.refs_6_ = bf16[96,896]{1,0:T(8,128)(2,1)S(1)} collective-permute-done((bf16[96,896]{1,0:T(8,128)(2,1)S(1)}, bf16[96,896]{1,0:T(8,128)(2,1)S(1)}, u32[]{:S(2)}, u32[]{:S(2)}) %collective-permute-start) | collective-permute-done | bytes 172064 | tf_op jit(solution)/shard_map/ppermute | solution.py:38
  26.2 5.2 %collective-permute-done.7.refs_8_ = bf16[96,896]{1,0:T(8,128)(2,1)S(1)} collective-permute-done((bf16[96,896]{1,0:T(8,128)(2,1)S(1)}, bf16[96,896]{1,0:T(8,128)(2,1)S(1)}, u32[]{:S(2)}, u32[]{:S(2)}) %collective-permute-start.7) | collective-permute-done | bytes 172064 | tf_op jit(solution)/shard_map/ppermute | solution.py:38
  35.7 6.4 %collective-permute-done.14.refs_2_.refs_10_ = bf16[512,768]{1,0:T(8,128)(2,1)} collective-permute-done((bf16[512,768]{1,0:T(8,128)(2,1)}, bf16[512,768]{1,0:T(8,128)(2,1)}, u32[]{:S(2)}, u32[]{:S(2)}) %collective-permute-start.14) | collective-permute-done | bytes 786464 | tf_op jit(solution)/shard_map/ppermute | solution.py:38
  53.1 8.6 %shard_map.222 = (bf16[2048,768]{1,0:T(8,128)(2,1)}, bf16[2048,192]{1,0:T(8,128)(2,1)}, bf16[2048,192]{1,0:T(8,128)(2,1)}, bf16[2048,192]{1,0:T(8,128)(2,1)}, bf...) custom-call(s32[8]{0:T(128)S(1)} %broadcast_xor_fusion.place_ref, ...), custom_call_target="tpu_custom_call" | custom-call | tf_op jit(solution)/shard_map/pallas_call | solution.py:266
  61.8 13.4 %shard_map.223 = (bf16[1024,192]{1,0:T(8,128)(2,1)S(1)}, f32[1024,3]{1,0:T(8,128)S(1)}) custom-call(s32[1,4]{1,0:T(1,128)S(1)} %copy-done.15, s32[1,4]{1,0:T(1,128)S(1)} %copy-done.16, s32[1]{0:T(128)} %bitcast.3.own_ref, bf16[2048,192]{1,0:T(8,128)(2,1)} %get-tuple-element.91.q_ref, bf16[2048,192]{1,0:T(8,128)(2,1)} %get-tuple-element.92.k_ref, ...), custom_call_target="tpu_custom_call" | custom-call | tf_op jit(solution)/shard_map/pallas_call | solution.py:411
  79.4 13.4 %shard_map.224 = (bf16[1024,192]{1,0:T(8,128)(2,1)S(1)}, f32[1024,3]{1,0:T(8,128)S(1)}) custom-call(s32[1,4]{1,0:T(1,128)S(1)} %copy-done.15, s32[1,4]{1,0:T(1,128)S(1)} %copy-done.16, s32[1]{0:T(128)} %bitcast.3.own_ref, bf16[2048,192]{1,0:T(8,128)(2,1)} %get-tuple-element.91.q_ref, bf16[2048,192]{1,0:T(8,128)(2,1)} %get-tuple-element.92.k_ref, ...), custom_call_target="tpu_custom_call" | custom-call | tf_op jit(solution)/shard_map/pallas_call | solution.py:411
  94.4 8.0 %collective-permute-done.25.refs_17_ = bf16[96,1536]{1,0:T(8,128)(2,1)S(1)} collective-permute-done((bf16[96,1536]{1,0:T(8,128)(2,1)S(1)}, bf16[96,1536]{1,0:T(8,128)(2,1)S(1)}, u32[]{:S(2)}, u32[]{:S(2)}) %collective-permute-start.25) | collective-permute-done | bytes 294944 | tf_op jit(solution)/shard_map/ppermute | solution.py:38
  104.7 16.3 %shard_map.225 = (bf16[512,768]{1,0:T(8,128)(2,1)}, bf16[512,768]{1,0:T(8,128)(2,1)}, bf16[512,768]{1,0:T(8,128)(2,1)}, bf16[512,768]{1,0:T(8,128)(2,1)}, bf16[1...) custom-call(s32[8]{0:T(128)S(1)} %broadcast_xor_fusion.place_ref, ...), custom_call_target="tpu_custom_call" | custom-call | tf_op jit(solution)/shard_map/pallas_call | solution.py:527
  129.8 16.0 %shard_map.226 = (bf16[512,768]{1,0:T(8,128)(2,1)}, bf16[512,768]{1,0:T(8,128)(2,1)}, bf16[512,768]{1,0:T(8,128)(2,1)}, bf16[512,768]{1,0:T(8,128)(2,1)}, bf16[1...) custom-call(s32[8]{0:T(128)S(1)} %broadcast_xor_fusion.place_ref, ...), custom_call_target="tpu_custom_call" | custom-call | tf_op jit(solution)/shard_map/pallas_call | solution.py:527
  148.4 17.7 %collective-permute-done.31 = bf16[512,768]{1,0:T(8,128)(2,1)S(1)} collective-permute-done((bf16[512,768]{1,0:T(8,128)(2,1)S(1)}, bf16[512,768]{1,0:T(8,128)(2,1)S(1)}, u32[]{:S(2)}, u32[]{:S(2)}) %collective-permute-start.31) | collective-permute-done | bytes 786464 | tf_op jit(solution)/shard_map/ppermute | solution.py:38
  170.6 17.4 %collective-permute-done.33.ga_ref.refs_2_ = bf16[512,768]{1,0:T(8,128)(2,1)S(1)} collective-permute-done((bf16[512,768]{1,0:T(8,128)(2,1)S(1)}, bf16[512,768]{1,0:T(8,128)(2,1)S(1)}, u32[]{:S(2)}, u32[]{:S(2)}) %collective-permute-start.33) | collective-permute-done | bytes 786464 | tf_op jit(solution)/shard_map/ppermute | solution.py:38
  188.0 12.5 %shard_map.232 = (bf16[96,1536]{1,0:T(8,128)(2,1)S(1)}, bf16[96,1536]{1,0:T(8,128)(2,1)S(1)}, bf16[96,1536]{1,0:T(8,128)(2,1)S(1)}, bf16[96,1536]{1,0:T(8,128)(2...) custom-call(s32[8]{0:T(128)S(1)} %broadcast_xor_fusion.place_ref, ...), custom_call_target="tpu_custom_call" | custom-call | tf_op jit(solution)/shard_map/pallas_call | solution.py:333
  202.1 21.9 %shard_map.227 = (bf16[1024,192]{1,0:T(8,128)(2,1)S(1)}, f32[192,2048]{1,0:T(8,128)}, f32[192,2048]{1,0:T(8,128)}) custom-call(s32[1,4]{1,0:T(1,128)S(1)} %copy-done.15, s32[1,4]{1,0:T(1,128)S(1)} %copy-done.16, s32[1]{0:T(128)} %bitcast.3.own_ref, bf16[2048,192]{1,0:T(8,128)(2,1)} %get-tuple-element.91.q_ref, bf16[2048,192]{1,0:T(8,128)(2,1)} %get-tuple-element.92.k_ref, ...), custom_call_target="tpu_custom_call" | custom-call | tf_op jit(solution)/shard_map/pallas_call | solution.py:466
  224.9 23.5 %shard_map.228 = (bf16[1024,192]{1,0:T(8,128)(2,1)S(1)}, bf16[2048,192]{1,0:T(8,128)(2,1)}, bf16[2048,192]{1,0:T(8,128)(2,1)}) custom-call(s32[1,4]{1,0:T(1,128)S(1)} %copy-done.15, s32[1,4]{1,0:T(1,128)S(1)} %copy-done.16, s32[1]{0:T(128)} %bitcast.3.own_ref, bf16[2048,192]{1,0:T(8,128)(2,1)} %get-tuple-element.91.q_ref, ...), custom_call_target="tpu_custom_call" | custom-call | tf_op jit(solution)/shard_map/pallas_call | solution.py:466
  249.2 7.0 %shard_map.231 = (bf16[96,576]{1,0:T(8,128)(2,1)S(1)}, bf16[96,576]{1,0:T(8,128)(2,1)S(1)}, bf16[96,576]{1,0:T(8,128)(2,1)S(1)}, bf16[96,576]{1,0:T(8,128)(2,1)S...) custom-call(s32[8]{0:T(128)S(1)} %broadcast_xor_fusion.place_ref, ...), custom_call_target="tpu_custom_call" | custom-call | tf_op jit(solution)/shard_map/pallas_call | solution.py:333
  282.5 12.3 %collective-permute-done.56.refs_2_ = bf16[96,1536]{1,0:T(8,128)(2,1)S(1)} collective-permute-done((bf16[96,1536]{1,0:T(8,128)(2,1)S(1)}, bf16[96,1536]{1,0:T(8,128)(2,1)S(1)}, u32[]{:S(2)}, u32[]{:S(2)}) %collective-permute-start.56) | collective-permute-done | bytes 294944 | tf_op jit(solution)/shard_map/ppermute | solution.py:38
  297.2 4.3 %shard_map.230 = (bf16[512,768]{1,0:T(8,128)(2,1)S(1)}, bf16[512,768]{1,0:T(8,128)(2,1)}) custom-call(bf16[1024,192]{1,0:T(8,128)(2,1)S(1)} %copy-done.8, bf16[2048,192]{1,0:T(8,128)(2,1)} %get-tuple-element.115.dk_ref.refs_5_, bf16[2048,192]{1,0:T(8,128)(2,1)} %get-tuple-element.116.dv_ref.refs_6_, bf16[768,896]{1,0:T(8,128)(2,1)} %get-tuple-element.117.w_ref.refs_0_), custom_call_target="tpu_custom_call" | custom-call | tf_op jit(solution)/shard_map/pallas_call | solution.py:552
  305.9 4.7 %shard_map.233 = (bf16[96,192]{1,0:T(8,128)(2,1)S(1)}, bf16[96,192]{1,0:T(8,128)(2,1)S(1)}, bf16[96,192]{1,0:T(8,128)(2,1)S(1)}, bf16[96,192]{1,0:T(8,128)(2,1)S...) custom-call(s32[8]{0:T(128)S(1)} %broadcast_xor_fusion.place_ref, bf16[512,768]{1,0:T(8,128)(2,1)} %copy-done.27, ...), custom_call_target="tpu_custom_call" | custom-call | tf_op jit(solution)/shard_map/pallas_call | solution.py:333
  318.5 5.5 %collective-permute-done.48 = bf16[288,576]{1,0:T(8,128)(2,1)S(1)} collective-permute-done((bf16[288,576]{1,0:T(8,128)(2,1)S(1)}, bf16[288,576]{1,0:T(8,128)(2,1)S(1)}, u32[]{:S(2)}, u32[]{:S(2)}) %collective-permute-start.48) | collective-permute-done | bytes 331808 | tf_op jit(solution)/shard_map/ppermute | solution.py:38
  326.0 6.9 %collective-permute-start.51 = (bf16[96,768]{1,0:T(8,128)(2,1)S(1)}, bf16[96,768]{1,0:T(8,128)(2,1)S(1)}, u32[]{:S(2)}, u32[]{:S(2)}) collective-permute-start(bf16[96,768]{1,0:T(8,128)(2,1)S(1)} %pad_maximum_fusion.2), channel_id=1, source_target_pairs={{0,16},{4,20},{8,24},{12,28},{16,0},{20,4},{24,8},{28,12},{1,17},{... | collective-permute-start | bytes 442376 | tf_op jit(solution)/shard_map/ppermute | solution.py:38
  333.9 6.8 %collective-permute-done.51.refs_2_ = bf16[96,768]{1,0:T(8,128)(2,1)S(1)} collective-permute-done((bf16[96,768]{1,0:T(8,128)(2,1)S(1)}, bf16[96,768]{1,0:T(8,128)(2,1)S(1)}, u32[]{:S(2)}, u32[]{:S(2)}) %collective-permute-start.51) | collective-permute-done | bytes 147488 | tf_op jit(solution)/shard_map/ppermute | solution.py:38
  340.8 5.0 %collective-permute-done.52.refs_3_ = bf16[96,768]{1,0:T(8,128)(2,1)S(1)} collective-permute-done((bf16[96,768]{1,0:T(8,128)(2,1)S(1)}, bf16[96,768]{1,0:T(8,128)(2,1)S(1)}, u32[]{:S(2)}, u32[]{:S(2)}) %collective-permute-start.52) | collective-permute-done | bytes 147488 | tf_op jit(solution)/shard_map/ppermute | solution.py:38
  348.1 5.1 %collective-permute-done.40 = bf16[512,768]{1,0:T(8,128)(2,1)S(1)} collective-permute-done((bf16[512,768]{1,0:T(8,128)(2,1)S(1)}, bf16[512,768]{1,0:T(8,128)(2,1)S(1)}, u32[]{:S(2)}, u32[]{:S(2)}) %collective-permute-start.40) | collective-permute-done | bytes 786464 | tf_op jit(solution)/shard_map/ppermute | solution.py:38
  (242 shorter events, 106.9 us)
Async XLA Ops:
  0.6 23.0 %collective-permute-start.5 = (bf16[512,768]{1,0:T(8,128)(2,1)}, bf16[512,768]{1,0:T(8,128)(2,1)}, u32[]{:S(2)}, u32[]{:S(2)}) collective-permute-start(bf16[512,768]{1,0:T(8,128)(2,1)} %refs_0_.5), channel_id=1, source_target_pairs={{0,2},{1,3},{2,0},{3,1},{4,6},{5,7},{6,4},{7,5},{8,10},{9,11},{10,... | collective-permute-start | bytes 2359304 | tf_op jit(solution)/shard_map/ppermute | solution.py:38
  23.2 18.9 %collective-permute-start.14 = (bf16[512,768]{1,0:T(8,128)(2,1)}, bf16[512,768]{1,0:T(8,128)(2,1)}, u32[]{:S(2)}, u32[]{:S(2)}) collective-permute-start(bf16[512,768]{1,0:T(8,128)(2,1)} %refs_8_), channel_id=1, source_target_pairs={{0,2},{1,3},{2,0},{3,1},{4,6},{5,7},{6,4},{7,5},{8,10},{9,11},{10,... | collective-permute-start | bytes 2359304 | tf_op jit(solution)/shard_map/ppermute | solution.py:38
  23.7 26.4 %collective-permute-start.1 = (bf16[512,768]{1,0:T(8,128)(2,1)}, bf16[512,768]{1,0:T(8,128)(2,1)S(1)}, u32[]{:S(2)}, u32[]{:S(2)}) collective-permute-start(bf16[512,768]{1,0:T(8,128)(2,1)} %refs_0_.5), channel_id=1, source_target_pairs={{0,1},{1,0},{2,3},{3,2},{4,5},{5,4},{6,7},{7,6},{8,9},{9,8},{10,11... | collective-permute-start | bytes 2359304 | tf_op jit(solution)/shard_map/ppermute | solution.py:38
  23.7 29.4 %collective-permute-start.6 = (bf16[512,768]{1,0:T(8,128)(2,1)}, bf16[512,768]{1,0:T(8,128)(2,1)}, u32[]{:S(2)}, u32[]{:S(2)}) collective-permute-start(bf16[512,768]{1,0:T(8,128)(2,1)} %collective-permute-done.5.refs_2_.refs_0_), channel_id=1, source_target_pairs={{0,1},{1,0},{2,3},{3,2},{4,5},{5,4},{6,7},{7,6},{8,9},{9,8},{10,11... | collective-permute-start | bytes 2359304 | tf_op jit(solution)/shard_map/ppermute | solution.py:38
  43.6 50.3 %collective-permute-start.18 = (bf16[512,768]{1,0:T(8,128)(2,1)}, bf16[512,768]{1,0:T(8,128)(2,1)}, u32[]{:S(2)}, u32[]{:S(2)}) collective-permute-start(bf16[512,768]{1,0:T(8,128)(2,1)} %collective-permute-done.14.refs_2_.refs_10_), channel_id=1, source_target_pairs={{0,1},{1,0},{2,3},{3,2},{4,5},{5,4},{6,7},{7,6},{8,9},{9,8},{10,11... | collective-permute-start | bytes 2359304 | tf_op jit(solution)/shard_map/ppermute | solution.py:38
  47.5 28.3 %collective-permute-start.23 = (bf16[96,1536]{1,0:T(8,128)(2,1)S(1)}, bf16[96,1536]{1,0:T(8,128)(2,1)S(1)}, u32[]{:S(2)}, u32[]{:S(2)}) collective-permute-start(bf16[96,1536]{1,0:T(8,128)(2,1)S(1)} %get-tuple-element.101.refs_13_), channel_id=1, source_target_pairs={{0,16},{4,20},{8,24},{12,28},{16,0},{20,4},{24,8},{28,12},{1,17},{... | collective-permute-start | bytes 884744 | tf_op jit(solution)/shard_map/ppermute | solution.py:38
  47.5 28.8 %collective-permute-start.22 = (bf16[96,1536]{1,0:T(8,128)(2,1)S(1)}, bf16[96,1536]{1,0:T(8,128)(2,1)S(1)}, u32[]{:S(2)}, u32[]{:S(2)}) collective-permute-start(bf16[96,1536]{1,0:T(8,128)(2,1)S(1)} %get-tuple-element.101.refs_13_), channel_id=1, source_target_pairs={{0,8},{4,12},{8,0},{12,4},{16,24},{20,28},{24,16},{28,20},{1,9},{5... | collective-permute-start | bytes 884744 | tf_op jit(solution)/shard_map/ppermute | solution.py:38
  51.0 26.9 %collective-permute-start.28 = (bf16[96,1536]{1,0:T(8,128)(2,1)S(1)}, bf16[96,1536]{1,0:T(8,128)(2,1)}, u32[]{:S(2)}, u32[]{:S(2)}) collective-permute-start(bf16[96,1536]{1,0:T(8,128)(2,1)S(1)} %collective-permute-done.24.refs_16_), channel_id=1, source_target_pairs={{0,4},{4,0},{8,12},{12,8},{16,20},{20,16},{24,28},{28,24},{1,5},{5... | collective-permute-start | bytes 884744 | tf_op jit(solution)/shard_map/ppermute | solution.py:38
  75.2 17.7 %collective-permute-start.20 = (bf16[1024,192]{1,0:T(8,128)(2,1)S(1)}, bf16[1024,192]{1,0:T(8,128)(2,1)S(1)}, u32[]{:S(2)}, u32[]{:S(2)}) collective-permute-start(bf16[1024,192]{1,0:T(8,128)(2,1)S(1)} %get-tuple-element.94.refs_4_.o_ref), channel_id=1, source_target_pairs={{0,2},{1,3},{2,0},{3,1},{4,6},{5,7},{6,4},{7,5},{8,10},{9,11},{10,... | collective-permute-start | bytes 1179656 | tf_op jit(solution)/shard_map/ppermute | solution.py:38
  102.4 19.3 %collective-permute-start.4 = (bf16[512,768]{1,0:T(8,128)(2,1)S(1)}, bf16[512,768]{1,0:T(8,128)(2,1)S(1)}, u32[]{:S(2)}, u32[]{:S(2)}) collective-permute-start(bf16[512,768]{1,0:T(8,128)(2,1)S(1)} %copy-done.25), channel_id=1, source_target_pairs={{0,1},{1,0},{2,3},{3,2},{4,5},{5,4},{6,7},{7,6},{8,9},{9,8},{10,11... | collective-permute-start | bytes 2359304 | tf_op jit(solution)/shard_map/ppermute | solution.py:38
  102.4 19.2 %collective-permute-start.12 = (bf16[1024,192]{1,0:T(8,128)(2,1)S(1)}, bf16[1024,192]{1,0:T(8,128)(2,1)S(1)}, u32[]{:S(2)}, u32[]{:S(2)}) collective-permute-start(bf16[1024,192]{1,0:T(8,128)(2,1)S(1)} %get-tuple-element.95.refs_4_.o_ref.refs_5_), channel_id=1, source_target_pairs={{0,2},{1,3},{2,0},{3,1},{4,6},{5,7},{6,4},{7,5},{8,10},{9,11},{10,... | collective-permute-start | bytes 1179656 | tf_op jit(solution)/shard_map/ppermute | solution.py:38
  121.0 25.0 %collective-permute-start.30 = (bf16[512,768]{1,0:T(8,128)(2,1)}, bf16[512,768]{1,0:T(8,128)(2,1)S(1)}, u32[]{:S(2)}, u32[]{:S(2)}) collective-permute-start(bf16[512,768]{1,0:T(8,128)(2,1)} %get-tuple-element.109), channel_id=1, source_target_pairs={{0,1},{1,0},{2,3},{3,2},{4,5},{5,4},{6,7},{7,6},{8,9},{9,8},{10,11... | collective-permute-start | bytes 2359304 | tf_op jit(solution)/shard_map/ppermute | solution.py:38
  146.2 19.9 %collective-permute-start.31 = (bf16[512,768]{1,0:T(8,128)(2,1)S(1)}, bf16[512,768]{1,0:T(8,128)(2,1)S(1)}, u32[]{:S(2)}, u32[]{:S(2)}) collective-permute-start(bf16[512,768]{1,0:T(8,128)(2,1)S(1)} %add_convert_fusion.2), channel_id=1, source_target_pairs={{0,2},{1,3},{2,0},{3,1},{4,6},{5,7},{6,4},{7,5},{8,10},{9,11},{10,... | collective-permute-start | bytes 2359304 | tf_op jit(solution)/shard_map/ppermute | solution.py:38
  169.1 18.9 %collective-permute-start.33 = (bf16[512,768]{1,0:T(8,128)(2,1)S(1)}, bf16[512,768]{1,0:T(8,128)(2,1)S(1)}, u32[]{:S(2)}, u32[]{:S(2)}) collective-permute-start(bf16[512,768]{1,0:T(8,128)(2,1)S(1)} %get-tuple-element.165.ga_ref.refs_0_), channel_id=1, source_target_pairs={{0,2},{1,3},{2,0},{3,1},{4,6},{5,7},{6,4},{7,5},{8,10},{9,11},{10,... | collective-permute-start | bytes 2359304 | tf_op jit(solution)/shard_map/ppermute | solution.py:38
  170.6 30.5 %collective-permute-start.32 = (bf16[512,768]{1,0:T(8,128)(2,1)S(1)}, bf16[512,768]{1,0:T(8,128)(2,1)S(1)}, u32[]{:S(2)}, u32[]{:S(2)}) collective-permute-start(bf16[512,768]{1,0:T(8,128)(2,1)S(1)} %get-tuple-element.165.ga_ref.refs_0_), channel_id=1, source_target_pairs={{0,1},{1,0},{2,3},{3,2},{4,5},{5,4},{6,7},{7,6},{8,9},{9,8},{10,11... | collective-permute-start | bytes 2359304 | tf_op jit(solution)/shard_map/ppermute | solution.py:38
  188.0 35.9 %collective-permute-start.34 = (bf16[512,768]{1,0:T(8,128)(2,1)S(1)}, bf16[512,768]{1,0:T(8,128)(2,1)S(1)}, u32[]{:S(2)}, u32[]{:S(2)}) collective-permute-start(bf16[512,768]{1,0:T(8,128)(2,1)S(1)} %collective-permute-done.33.ga_ref.refs_2_), channel_id=1, source_target_pairs={{0,1},{1,0},{2,3},{3,2},{4,5},{5,4},{6,7},{7,6},{8,9},{9,8},{10,11... | collective-permute-start | bytes 2359304 | tf_op jit(solution)/shard_map/ppermute | solution.py:38
  200.5 69.2 %collective-permute-start.54 = (bf16[288,1536]{1,0:T(8,128)(2,1)}, bf16[288,1536]{1,0:T(8,128)(2,1)}, u32[]{:S(2)}, u32[]{:S(2)}) collective-permute-start(bf16[288,1536]{1,0:T(8,128)(2,1)} %get-tuple-element.157), channel_id=1, source_target_pairs={{0,4},{4,0},{8,12},{12,8},{16,20},{20,16},{24,28},{28,24},{1,5},{5... | collective-permute-start | bytes 2654216 | tf_op jit(solution)/shard_map/ppermute | solution.py:38
  271.3 23.5 %collective-permute-start.56 = (bf16[96,1536]{1,0:T(8,128)(2,1)S(1)}, bf16[96,1536]{1,0:T(8,128)(2,1)S(1)}, u32[]{:S(2)}, u32[]{:S(2)}) collective-permute-start(bf16[96,1536]{1,0:T(8,128)(2,1)S(1)} %get-tuple-element.168), channel_id=1, source_target_pairs={{0,16},{4,20},{8,24},{12,28},{16,0},{20,4},{24,8},{28,12},{1,17},{... | collective-permute-start | bytes 884744 | tf_op jit(solution)/shard_map/ppermute | solution.py:38
  273.7 21.1 %collective-permute-start.55 = (bf16[96,1536]{1,0:T(8,128)(2,1)S(1)}, bf16[96,1536]{1,0:T(8,128)(2,1)S(1)}, u32[]{:S(2)}, u32[]{:S(2)}) collective-permute-start(bf16[96,1536]{1,0:T(8,128)(2,1)S(1)} %get-tuple-element.169), channel_id=1, source_target_pairs={{0,24},{4,28},{8,16},{12,20},{16,8},{20,12},{24,0},{28,4},{1,25},{... | collective-permute-start | bytes 884744 | tf_op jit(solution)/shard_map/ppermute | solution.py:38
  279.4 33.9 %collective-permute-start.45 = (f32[2,768]{1,0:T(2,128)S(1)}, f32[2,768]{1,0:T(2,128)S(1)}, u32[]{:S(2)}, u32[]{:S(2)}) collective-permute-start(f32[2,768]{1,0:T(2,128)S(1)} %add.123), channel_id=1, source_target_pairs={{0,1},{1,0},{2,3},{3,2},{4,5},{5,4},{6,7},{7,6},{8,9},{9,8},{10,11... | collective-permute-start | bytes 18440 | tf_op jit(solution)/shard_map/ppermute | solution.py:38
  295.7 51.0 %collective-permute-start.37 = (bf16[512,768]{1,0:T(8,128)(2,1)S(1)}, bf16[512,768]{1,0:T(8,128)(2,1)S(1)}, u32[]{:S(2)}, u32[]{:S(2)}) collective-permute-start(bf16[512,768]{1,0:T(8,128)(2,1)S(1)} %convert_add_fusion), channel_id=1, source_target_pairs={{0,2},{1,3},{2,0},{3,1},{4,6},{5,7},{6,4},{7,5},{8,10},{9,11},{10,... | collective-permute-start | bytes 2359304 | tf_op jit(solution)/shard_map/ppermute | solution.py:38
  312.7 20.4 %collective-permute-start.46 = (bf16[96,576]{1,0:T(8,128)(2,1)S(1)}, bf16[96,576]{1,0:T(8,128)(2,1)S(1)}, u32[]{:S(2)}, u32[]{:S(2)}) collective-permute-start(bf16[96,576]{1,0:T(8,128)(2,1)S(1)} %copy-done.20), channel_id=1, source_target_pairs={{0,4},{4,0},{8,12},{12,8},{16,20},{20,16},{24,28},{28,24},{1,5},{5... | collective-permute-start | bytes 331784 | tf_op jit(solution)/shard_map/ppermute | solution.py:38
  318.5 28.2 %collective-permute-start.35 = (bf16[512,768]{1,0:T(8,128)(2,1)S(1)}, bf16[512,768]{1,0:T(8,128)(2,1)S(1)}, u32[]{:S(2)}, u32[]{:S(2)}) collective-permute-start(bf16[512,768]{1,0:T(8,128)(2,1)S(1)} %copy-done.47), channel_id=1, source_target_pairs={{0,1},{1,0},{2,3},{3,2},{4,5},{5,4},{6,7},{7,6},{8,9},{9,8},{10,11... | collective-permute-start | bytes 2359304 | tf_op jit(solution)/shard_map/ppermute | solution.py:38
  333.3 19.9 %collective-permute-start.40 = (bf16[512,768]{1,0:T(8,128)(2,1)S(1)}, bf16[512,768]{1,0:T(8,128)(2,1)S(1)}, u32[]{:S(2)}, u32[]{:S(2)}) collective-permute-start(bf16[512,768]{1,0:T(8,128)(2,1)S(1)} %add_convert_fusion), channel_id=1, source_target_pairs={{0,2},{1,3},{2,0},{3,1},{4,6},{5,7},{6,4},{7,5},{8,10},{9,11},{10,... | collective-permute-start | bytes 2359304 | tf_op jit(solution)/shard_map/ppermute | solution.py:38
  (84 other events, 766.6 us)
